TPU v7x, 32 devices: a whole 2x2x4 slice. The times are simulated.
32 devices in a mesh: member: 4 (over z), region: 4 (over y, x), fine: 2 (over core).
Axes of the slice: x: 2, y: 2, z: 4, core: 2. Of those that a mesh axis runs over, the one named last changes fastest.
Arguments:
- sample_surface_elevation: float32 [256, 4, 512], P('member', 'region', 'fine'), may hold values from -6 to 6
- sample_zonal_current: float32 [256, 4, 512], P('member', 'region', 'fine'), may hold values from -6 to 6
- sample_meridional_current: float32 [256, 4, 512], P('member', 'region', 'fine'), may hold values from -6 to 6
- zonal_edge_layer_courant: float32 [4, 512], P('region', 'fine'), may hold values from 0.1 to 0.45
- meridional_edge_layer_courant: float32 [4, 512], P('region', 'fine'), may hold values from 0.1 to 0.45
- obs_index: int32 [64, 512, 4], P(('member', 'region', 'fine')), may hold values from 0 to 95
- obs_weight: float32 [64, 512, 4], P(('member', 'region', 'fine')), may hold values from 0.1 to 1
- obs_value: float32 [64, 512], P(('member', 'region', 'fine')), may hold values from -12 to 12
- obs_var: float32 [64, 512], P(('member', 'region', 'fine')), may hold values from 0.25 to 4
- obs_count: int32 [64], P(('member', 'region', 'fine')), may hold values from 64 to 512, as said below
- fine_ctrl: float32 [3, 8, 2, 512], P(None, 'region', 'fine', 'member'), may hold values from -6 to 6
Outputs:
- ana_h: float32 [256, 4, 512], P('member', 'region', 'fine')
- ana_u: float32 [256, 4, 512], P('member', 'region', 'fine')
- ana_v: float32 [256, 4, 512], P('member', 'region', 'fine')
- fine_out: float32 [3, 8, 2, 512], P(None, 'region', 'fine', 'member')
Inputs may be any that keep to these rules, and one draw needn't show every extreme that they name: `obs_count`: each region's count is 512 // 8 times 1, 2, 4 or 8; some region has 512 and some 512 // 8 in every draw; the live observations of a region are its first count slots.
All inputs are finite; a program needn't handle non-finite values.
Results may differ from a plain program's by a relative error of at most 0.0003.
Values sent between devices are 32-bit elements; how exact they have to be, the bound alone decides.
No kernel may reach another device: no remote copies, remote signals or barrier semaphores. Data moves between devices by JAX's collectives and lax.ppermute only.
A program may use at most 64 MiB of HBM per device.

v0:
```python
import functools

import jax
import jax.numpy as jnp
from jax import lax
from jax.experimental import pallas as pl
from jax.experimental.pallas import tpu as pltpu
from jax.sharding import PartitionSpec as P


REG_DEV = 2
STEPS = 4
NEWTON = 8
LANES = 128
TILE = 8
HALF = LANES // 2
GRANT = 32 << 20


HIGHEST = lax.Precision.HIGHEST
NT = (((1,), (1,)), ((), ()))
NN = (((1,), (0,)), ((), ()))
VMEM = pl.BlockSpec(memory_space=pltpu.VMEM)
SMEM = pl.BlockSpec(memory_space=pltpu.SMEM)
HBM = pl.BlockSpec(memory_space=pltpu.HBM)


def passed_along(block, axis, distance):
    count = lax.axis_size(axis)
    route = [((i - distance) % count, i) for i in range(count)]
    return lax.ppermute(block, axis, route)


def lane_of(shape):
    return lax.broadcasted_iota(jnp.int32, shape, 1)


def row_of(shape):
    return lax.broadcasted_iota(jnp.int32, shape, 0)


def swapped(tile):
    return pltpu.roll(tile, HALF, 1)


def low_pair(even, odd):
    return jnp.where(lane_of(even.shape) < HALF, even, swapped(odd))


def high_pair(even, odd):
    return jnp.where(lane_of(even.shape) < HALF, swapped(even), odd)


def split(value):
    high = value.astype(jnp.bfloat16)
    return high, (value - high.astype(jnp.float32)).astype(jnp.bfloat16)


def beside(value):
    return jnp.concatenate(split(value), axis=1)


def stacked(value):
    both = jnp.concatenate(split(value), axis=1)
    return jnp.concatenate([both, both], axis=0)


def times(left, right):
    out = lax.dot_general(left, right, NN, preferred_element_type=jnp.float32)
    half = out.shape[1] // 2
    return out[:, :half] + out[:, half:]


def squared(value):
    both = jnp.concatenate(split(value), axis=0)
    out = lax.dot_general(both, both, NT, preferred_element_type=jnp.float32)
    half = out.shape[0] // 2
    out = out[:, :half] + out[:, half:]
    return out[:half] + out[half:]


BACK_ROWS = 3 * TILE + 1


def turn_kernel(mem, later, *refs):
    sources, refs = refs[: 6 + later], refs[6 + later :]
    pair_ref, single_ref, edge_ref, live_ref = refs[:4]
    targets, sems = refs[4 + later : -1] + refs[4 : 4 + later], refs[-1]
    copies = [
        pltpu.make_async_copy(source, target, sems.at[i])
        for i, (source, target) in enumerate(zip(sources, targets))
    ]
    for copy in copies:
        copy.start()
    h_ref, u_ref, v_ref, zonal_ref, merid_ref, count_ref = targets[:6]
    tiles = h_ref.shape[0] // mem
    columns = tiles * LANES
    zero = jnp.zeros((TILE, LANES), jnp.float32)
    for ref in (pair_ref, single_ref):
        ref[0:TILE, :] = zero
        ref[columns : columns + TILE, :] = zero
    for copy in copies[:5]:
        copy.wait()
    for t in range(tiles):
        rows = pl.ds(t, mem, stride=tiles)
        lanes = slice(t * LANES, (t + 1) * LANES)
        pair = jnp.concatenate([h_ref[rows, :], u_ref[rows, :]], axis=0)
        zonal = jnp.broadcast_to(zonal_ref[:, lanes], (mem // 2, LANES))
        merid = jnp.broadcast_to(merid_ref[:, lanes], (mem // 2, LANES))
        single = jnp.concatenate([v_ref[rows, :], zonal, merid], axis=0)
        place = slice(STEPS + t * LANES, STEPS + (t + 1) * LANES)
        pair_ref[place, :] = pair.T
        single_ref[place, :] = single.T
    early = row_of((TILE, LANES)) < STEPS
    for i, ref in enumerate((pair_ref, single_ref)):
        edge_ref[i] = jnp.where(early, ref[columns : columns + TILE, :], ref[0:TILE, :])
    for copy in copies[5:]:
        copy.wait()
    for q in range(REG_DEV):
        live_ref[q] = jnp.full(live_ref.shape[1:], count_ref[q], jnp.int32)


def blocks_kernel(groups, strips, width, pair_ref, single_ref, west_ref, east_ref, *refs):
    send_refs = refs[-strips:]
    me = lax.axis_index("region")
    shape = (TILE, LANES)
    early = row_of(shape) < STEPS
    part = lane_of(shape) % (HALF // 2)
    span = 3 * TILE
    for s, send_ref in enumerate(send_refs):
        owner = me ^ s
        first, last = early & (owner == 0), ~early & (owner == strips - 1)
        courant = jnp.zeros(shape, jnp.float32)
        for p in range(groups // 2):
            for j in range(3):
                pairs, singles = [], []
                for group in (2 * p, 2 * p + 1):
                    start = pl.multiple_of(width * (group * strips + owner) + TILE * j, TILE)
                    pair = pair_ref[pl.ds(start, TILE), :]
                    single = single_ref[pl.ds(start, TILE), :]
                    if group == 0 and j == 0:
                        pair = jnp.where(first, west_ref[0], pair)
                        single = jnp.where(first, west_ref[1], single)
                    if group == groups - 1 and j == 2:
                        pair = jnp.where(last, east_ref[0], pair)
                        single = jnp.where(last, east_ref[1], single)
                    pairs.append(pair)
                    singles.append(single)
                    courant = jnp.where(part == 3 * group + j, single, courant)
                place = 3 * span * p + TILE * j
                send_ref[place : place + TILE, :] = low_pair(*pairs)
                send_ref[place + span : place + span + TILE, :] = high_pair(*pairs)
                send_ref[place + 2 * span : place + 2 * span + TILE, :] = low_pair(*singles)
        place = 3 * span * (groups // 2)
        send_ref[place : place + TILE, :] = courant


def forecast_kernel(groups, strips, width, *refs):
    got_refs, refs = refs[:strips], refs[strips:]
    send_refs, (got_ref, turned_ref) = refs[:groups], refs[groups:]
    span = width + 2 * STEPS
    per_region = strips // REG_DEV
    cells = per_region * width
    me = lax.axis_index("region")
    for s, ref in enumerate(got_refs):
        got_ref[me ^ s] = ref[...]
    low = lane_of((TILE, LANES)) < HALF
    tail = 3 * span * (groups // 2)
    for p in range(groups // 2):

        def field(r, i):
            return got_ref[r, 3 * span * p + span * i : 3 * span * p + span * (i + 1), :]

        def courant(r, first):
            mixed = got_ref[r, tail : tail + TILE, :]
            parts = []
            for j in range(3):
                even, odd = first + 6 * p + j, first + 6 * p + 3 + j
                parts.append(
                    jnp.where(
                        low,
                        jnp.broadcast_to(mixed[:, even : even + 1], (TILE, LANES)),
                        jnp.broadcast_to(mixed[:, odd : odd + 1], (TILE, LANES)),
                    )
                )
            return jnp.concatenate(parts, axis=0)

        h = [field(r, 0) for r in range(strips)]
        u = [field(r, 1) for r in range(strips)]
        v = [field(r, 2) for r in range(strips)]
        zonal = [courant(r, HALF) for r in range(strips)]
        merid = [courant(r, HALF + HALF // 2) for r in range(strips)]
        for _ in range(STEPS):
            flux_v = [merid[r] * v[r] for r in range(strips)]
            for r in range(strips):
                flux_u = zonal[r] * u[r]
                south = flux_v[r - 1] if r else jnp.zeros_like(flux_u)
                h[r] = h[r] - (flux_u - pltpu.roll(flux_u, 1, 0) + flux_v[r] - south)
            for r in range(strips):
                north = h[r + 1] if r + 1 < strips else jnp.zeros_like(h[r])
                u[r] = u[r] - (pltpu.roll(h[r], span - 1, 0) - h[r])
                v[r] = v[r] - (north - h[r])
        for i, state in enumerate((h, u, v)):
            inner = [pltpu.roll(state[r], span - STEPS, 0)[:width] for r in range(strips)]
            for s in range(per_region):
                lower, upper = inner[s], inner[per_region + s]
                place = slice(i * cells + s * width, i * cells + (s + 1) * width)
                turned_ref[2 * p, place, :] = low_pair(lower, upper)
                turned_ref[2 * p + 1, place, :] = high_pair(lower, upper)
    mine = lax.axis_index("member")
    for s, ref in enumerate(send_refs):
        ref[...] = turned_ref[mine ^ s]


def collect(got_refs, all_ref, x_ref):
    states = all_ref.shape[1]
    mine = lax.axis_index("member")
    for s, ref in enumerate(got_refs):
        all_ref[mine ^ s] = ref[...]
    for p in range(len(got_refs) // 2):
        even, odd = all_ref[2 * p], all_ref[2 * p + 1]
        lanes = slice(p * LANES, (p + 1) * LANES)
        x_ref[0, :states, lanes] = low_pair(even, odd)
        x_ref[1, :states, lanes] = high_pair(even, odd)


def observe_kernel(live_ref, index_ref, weight_ref, value_ref, var_ref, info_ref, pull_ref):
    states = info_ref.shape[1]
    obs = index_ref.shape[2]
    for q in range(REG_DEV):
        state = row_of((states, obs))
        operator = jnp.zeros((states, obs), jnp.float32)
        for j in range(index_ref.shape[1]):
            hit = state == index_ref[q, j : j + 1, :]
            operator = operator + jnp.where(hit, weight_ref[q, j : j + 1, :], 0.0)
        live = lane_of((1, obs)) < live_ref[q, 0:1, 0:1]
        inverse = jnp.where(live, 1.0 / var_ref[q : q + 1, :], 0.0)
        scaled = operator * inverse
        info_ref[q] = lax.dot_general(
            scaled, operator, NT, precision=HIGHEST, preferred_element_type=jnp.float32
        )
        pulled = jnp.sum(scaled * value_ref[q : q + 1, :], axis=1, keepdims=True)
        pull_ref[q] = jnp.broadcast_to(pulled, (states, LANES))


def analyse(members, x_ref, info_ref, pull_ref, out_ref):
    states = x_ref.shape[1]
    square = (states, states)
    diagonal = row_of(square) == lane_of(square)
    identity = jnp.where(diagonal, 1.0, 0.0)
    regions = range(REG_DEV)
    scale = 1.0 / (members - 1)

    def as_row(column):
        return jnp.sum(jnp.where(diagonal, column, 0.0), axis=0, keepdims=True)

    def applied(matrix, row):
        return jnp.sum(matrix * row, axis=1, keepdims=True)

    x = [x_ref[q] for q in regions]
    means = [jnp.sum(x[q], axis=1, keepdims=True) / members for q in regions]
    spreads = [x[q] - means[q] for q in regions]
    covs = [squared(spreads[q]) for q in regions]
    gains = [times(beside(covs[q]), stacked(info_ref[q] * scale)) for q in regions]
    rights = [stacked(gains[q]) for q in regions]
    gains_2 = [times(beside(gains[q]), rights[q]) for q in regions]
    pulls, inverse_norms, iterates, inverses = [], [], [], []
    for q in regions:
        pulled = pull_ref[q][:, 0:1] - applied(info_ref[q], as_row(means[q]))
        pulls.append(jnp.sum(covs[q] * pulled, axis=0, keepdims=True))
        trace = jnp.sum(jnp.where(diagonal, gains_2[q] + 2.0 * gains[q], 0.0), keepdims=True)
        inverse_norms.append(lax.rsqrt(trace + members))
    for q in regions:
        norm = inverse_norms[q]
        first = (identity + gains[q]) * norm
        second = (identity + 2.0 * gains[q] + gains_2[q]) * (norm * norm)
        third = (second + times(beside(second), rights[q])) * norm
        inverses.append(1.5 * identity - 0.5 * first)
        iterates.append(2.25 * first - 1.5 * second + 0.25 * third)
    for _ in range(1, NEWTON - 1):
        rights = [stacked(iterates[q]) for q in regions]
        lefts = [
            jnp.concatenate([beside(iterates[q]), beside(inverses[q])], axis=0) for q in regions
        ]
        both = [times(lefts[q], rights[q]) for q in regions]
        seconds = [both[q][:states] for q in regions]
        thirds = [times(beside(seconds[q]), rights[q]) for q in regions]
        inverses = [1.5 * inverses[q] - 0.5 * both[q][states:] for q in regions]
        iterates = [
            2.25 * iterates[q] - 1.5 * seconds[q] + 0.25 * thirds[q] for q in regions
        ]
    increments = []
    for q in regions:
        high, low = split(spreads[q])
        wide = beside(inverses[q])
        moved = lax.dot_general(
            wide, jnp.concatenate([high, high], axis=0), NN, preferred_element_type=jnp.float32
        )
        moved = moved + lax.dot_general(
            wide[:, :states], low, NN, preferred_element_type=jnp.float32
        )
        twice = applied(inverses[q], as_row(applied(inverses[q], pulls[q])))
        factor = 1.5 * identity - 0.5 * iterates[q]
        twice = applied(factor, as_row(applied(factor, as_row(twice))))
        increment = twice * (inverse_norms[q] * scale)
        increments.append(increment)
        high, low = split(moved * jnp.sqrt(inverse_norms[q]))
        wide = beside(factor)
        moved = lax.dot_general(
            wide, jnp.concatenate([high, high], axis=0), NN, preferred_element_type=jnp.float32
        )
        moved = moved + lax.dot_general(
            wide[:, :states], low, NN, preferred_element_type=jnp.float32
        )
        out_ref[q] = moved + (means[q] + increment)
    return increments


def pack(groups, strips, width, ana_ref, increments, send_ref):
    per_region = strips // REG_DEV
    cells = per_region * width
    states = increments[0].shape[0]
    state = row_of((states, LANES))
    lane = lane_of((states, LANES))
    for r in range(strips):
        q, s = divmod(r, per_region)
        wanted = (lane // width) * cells + s * width + lane % width
        hit = (state == wanted) & (lane < 3 * width)
        row = jnp.sum(jnp.where(hit, increments[q], 0.0), axis=0, keepdims=True)
        for group in range(groups):
            block = group * strips + r
            lanes = slice((group // 2) * LANES, (group // 2 + 1) * LANES)
            pair = high_pair if group % 2 else low_pair
            for i in range(3):
                first = i * cells + s * width
                tile = pair(
                    ana_ref[q, first : first + TILE, lanes],
                    ana_ref[q, first + TILE : first + 2 * TILE, lanes],
                )
                send_ref[BACK_ROWS * block + TILE * i : BACK_ROWS * block + TILE * (i + 1), :] = tile
            send_ref[BACK_ROWS * (block + 1) - 1 : BACK_ROWS * (block + 1), :] = row


def region_kernel(groups, strips, width, *refs):
    got_refs, (info_ref, pull_ref, send_ref, all_ref, x_ref, ana_ref) = refs[:groups], refs[groups:]
    states = all_ref.shape[1]
    if states < x_ref.shape[1]:
        x_ref[:, states:, :] = jnp.zeros_like(x_ref[:, states:, :])
    collect(got_refs, all_ref, x_ref)
    increments = analyse(x_ref.shape[2], x_ref, info_ref, pull_ref, ana_ref)
    pack(groups, strips, width, ana_ref, increments, send_ref)


def home_kernel(mem, strips, width, got_ref, ctrl_ref, h_ref, u_ref, v_ref, fine_ref):
    tiles = got_ref.shape[0] // BACK_ROWS * width // LANES
    per_tile = LANES // width
    for i, out_ref in enumerate((h_ref, u_ref, v_ref)):
        for t in range(0, tiles, 2):
            rows = []
            for k in range(per_tile):
                first = BACK_ROWS * (t * per_tile + k) + TILE * i
                even = got_ref[first : first + TILE, :]
                first += BACK_ROWS * per_tile
                odd = got_ref[first : first + TILE, :]
                rows += [low_pair(even, odd), high_pair(even, odd)]
            turned = jnp.concatenate(rows, axis=0).T
            out_ref[pl.ds(t, mem, stride=tiles), :] = turned[:mem]
            out_ref[pl.ds(t + 1, mem, stride=tiles), :] = turned[mem:]
    mine = lax.axis_index("member") * strips
    per_fine = LANES // (2 * width)
    row = row_of((width, LANES))
    lane = lane_of((width, LANES))
    for t in range(ctrl_ref.shape[3] // LANES):
        rows = [
            got_ref[pl.ds(BACK_ROWS * (mine + t * per_fine + b) + BACK_ROWS - 1, 1), :]
            for b in range(per_fine)
        ]
        columns = [jnp.broadcast_to(r, (LANES, LANES)).T[:, 0:1] for r in rows]
        for i in range(3):
            total = jnp.zeros((1, LANES), jnp.float32)
            for b in range(per_fine):
                hit = ((lane // 2) % width == row) & (lane // (2 * width) == b)
                part = jnp.where(hit, columns[b][i * width : (i + 1) * width], 0.0)
                total = total + jnp.sum(part, axis=0, keepdims=True)
            lanes = slice(t * LANES, (t + 1) * LANES)
            for e in range(2):
                fine_ref[i, e, :, lanes] = ctrl_ref[i, e, :, lanes] + total


def collect_kernel(groups, *refs):
    collect(refs[:groups], refs[-1], refs[-2])


def pack_kernel(groups, strips, width, ana_ref, inc_ref, send_ref):
    pack(groups, strips, width, ana_ref, [inc_ref[q] for q in range(REG_DEV)], send_ref)


def analyse_in_members(x, obs_index, obs_weight, obs_value, obs_var, obs_count):
    states, members = x.shape[1:]
    mean_state = jnp.mean(x, axis=2, keepdims=True)
    spread = x - mean_state
    picks = (obs_index[:, :, :, None] == jnp.arange(states)).astype(jnp.float32)
    operator = jnp.sum(picks * obs_weight[:, :, :, None], axis=2)
    predicted = jnp.einsum("ros,rsk->rko", operator, x, precision=HIGHEST)
    mean_obs = jnp.mean(predicted, axis=1, keepdims=True)
    obs_spread = predicted - mean_obs
    active_obs = jnp.arange(obs_value.shape[1])[None, :] < obs_count[:, None]
    weighted = obs_spread * (active_obs.astype(jnp.float32) / obs_var)[:, None, :]
    gram_sum = jnp.einsum("rko,rjo->rkj", weighted, obs_spread, precision=HIGHEST)
    identity = jnp.eye(members, dtype=jnp.float32)
    scaled = identity + gram_sum / (members - 1)
    frobenius = jnp.sqrt(jnp.sum(scaled * scaled, axis=(1, 2), keepdims=True))
    iterate = scaled / frobenius
    inverse_root = jnp.broadcast_to(identity, scaled.shape)
    dot = functools.partial(jnp.einsum, "rij,rjk->rik", precision=HIGHEST)
    for _ in range(NEWTON):
        factor = 1.5 * identity - 0.5 * dot(inverse_root, iterate)
        iterate = dot(iterate, factor)
        inverse_root = dot(factor, inverse_root)
    transform = inverse_root / jnp.sqrt(frobenius)
    innovation = jnp.einsum(
        "rko,ro->rk", weighted, obs_value - mean_obs[:, 0], precision=HIGHEST
    )
    halfway = jnp.einsum("rkj,rj->rk", transform, innovation, precision=HIGHEST)
    mean_weights = jnp.einsum("rkj,rj->rk", transform, halfway, precision=HIGHEST) / (members - 1)
    increment = jnp.einsum("rk,rsk->rs", mean_weights, spread, precision=HIGHEST)[:, :, None]
    moved = jnp.einsum("rjk,rsj->rsk", transform, spread, precision=HIGHEST)
    return mean_state + increment + moved, increment


def call(kernel, out_shape, specs, scratch=(), cost=None):
    many = isinstance(out_shape, tuple)
    return pl.pallas_call(
        kernel,
        out_shape=out_shape,
        in_specs=specs,
        out_specs=tuple(VMEM for _ in out_shape) if many else VMEM,
        scratch_shapes=scratch,
        cost_estimate=cost,
        compiler_params=pltpu.CompilerParams(vmem_limit_bytes=GRANT),
    )


def swapped_blocks(blocks, axis):
    count = len(blocks)
    if count <= 4:
        routes = [[(i, i ^ s) for i in range(count)] for s in range(count)]
        moved = []
        for s in range(1, count):
            moved.append(lax.ppermute(blocks[s], axis, routes[s]))
        return [kept(block) for block in [blocks[0], *moved]]
    order = lax.axis_index(axis) ^ jnp.arange(count)
    moved = lax.all_to_all(jnp.stack(blocks)[order], axis, split_axis=0, concat_axis=0, tiled=True)
    return [kept(block) for block in moved[order]]


def exchanged(blocks, axes, count):
    dense = blocks.reshape(count, -1, 1, LANES)
    return lax.all_to_all(dense, axes, split_axis=0, concat_axis=0, tiled=True).reshape(blocks.shape)


def f32(*shape):
    return jax.ShapeDtypeStruct(shape, jnp.float32)


def near(*shape):
    return pltpu.VMEM(shape, jnp.float32)


def far(array):
    return pltpu.with_memory_space_constraint(array, pltpu.HBM)


def kept(array):
    return pltpu.with_memory_space_constraint(array, pltpu.VMEM)


def shards(
    sample_surface_elevation,
    sample_zonal_current,
    sample_meridional_current,
    zonal_edge_layer_courant,
    meridional_edge_layer_courant,
    obs_index,
    obs_weight,
    obs_value,
    obs_var,
    obs_count,
    fine_ctrl,
):
    groups = lax.axis_size("member")
    strips = lax.axis_size("region")
    owners = ("member", "region")
    mem, rows, columns = sample_surface_elevation.shape
    count = groups * strips
    width = columns // count
    members = groups * mem
    assert rows == 1 and 2 * mem == LANES and width == 2 * TILE and STEPS * 2 == TILE
    assert columns % (2 * LANES) == 0 and strips % REG_DEV == 0 and REG_DEV == 2
    assert all(size > 1 and size & (size - 1) == 0 for size in (groups, strips))
    assert 3 * groups <= HALF // 2
    flat = (mem * columns // LANES, LANES)
    states = 3 * width * strips // REG_DEV
    small = states <= members
    later = [fine_ctrl]
    if small:
        later += [obs_index.transpose(0, 2, 1), obs_weight.transpose(0, 2, 1), obs_value, obs_var]
    pair, single, edge, live, ctrl, *seen = call(
        functools.partial(turn_kernel, mem, len(later)),
        (
            near(columns + TILE, LANES),
            near(columns + TILE, LANES),
            near(2, TILE, LANES),
            pltpu.VMEM((REG_DEV, TILE, LANES), jnp.int32),
            *(pltpu.VMEM(array.shape, array.dtype) for array in later),
        ),
        [HBM] * (6 + len(later)),
        scratch=[
            *[pltpu.VMEM(flat, jnp.float32)] * 3,
            *[pltpu.VMEM((1, columns), jnp.float32)] * 2,
            pltpu.SMEM((REG_DEV,), jnp.int32),
            pltpu.SemaphoreType.DMA((6 + len(later),)),
        ],
    )(
        far(sample_surface_elevation.reshape(flat)),
        far(sample_zonal_current.reshape(flat)),
        far(sample_meridional_current.reshape(flat)),
        far(zonal_edge_layer_courant),
        far(meridional_edge_layer_courant),
        far(obs_count),
        *(far(array) for array in later),
    )
    from_west = passed_along(edge, "fine", 1)
    from_east = from_west if lax.axis_size("fine") == 2 else passed_along(edge, "fine", -1)
    ahead = []
    if small:
        padded = -(-states // LANES) * LANES
        obs = obs_value.shape[1]
        info, pull = call(
            observe_kernel,
            (near(REG_DEV, padded, padded), near(REG_DEV, padded, LANES)),
            [VMEM] * 5,
            cost=pl.CostEstimate(
                flops=12 * REG_DEV * padded * padded * obs, bytes_accessed=1 << 20, transcendentals=0
            ),
        )(kept(live), *(kept(array) for array in seen))
        ahead = [kept(pull)]
    layout = (groups, strips, width)
    span = width + 2 * STEPS
    out = call(
        functools.partial(blocks_kernel, *layout),
        tuple([near(3 * span * (groups // 2) + TILE, LANES)] * strips),
        [VMEM] * (4 + len(ahead)),
    )(kept(pair), kept(single), kept(from_west), kept(from_east), *ahead)
    got = swapped_blocks(out, "region")
    turned = call(
        functools.partial(forecast_kernel, *layout),
        tuple([near(states, LANES)] * groups),
        [VMEM] * strips,
        scratch=[
            pltpu.VMEM((strips, *out[0].shape), jnp.float32),
            pltpu.VMEM((groups, states, LANES), jnp.float32),
        ],
    )(*got)
    got = swapped_blocks(turned, "member")
    back_shape = near(count * BACK_ROWS, LANES)
    gathered = pltpu.VMEM((groups, states, LANES), jnp.float32)
    if small:
        back = call(
            functools.partial(region_kernel, *layout),
            back_shape,
            [VMEM] * (groups + 2),
            scratch=[
                gathered,
                pltpu.VMEM((REG_DEV, padded, members), jnp.float32),
                pltpu.VMEM((REG_DEV, padded, members), jnp.float32),
            ],
        )(*got, kept(info), kept(pull))
    else:
        x = call(
            functools.partial(collect_kernel, groups),
            f32(REG_DEV, states, members),
            [VMEM] * groups,
            scratch=[gathered],
        )(*got)
        analysis, increment = analyse_in_members(
            x, obs_index, obs_weight, obs_value, obs_var, obs_count
        )
        back = call(
            functools.partial(pack_kernel, *layout), back_shape, [VMEM] * 2
        )(analysis, increment)
    home = exchanged(back, owners, count)
    ana_h, ana_u, ana_v, fine_out = call(
        functools.partial(home_kernel, mem, strips, width),
        (f32(*flat), f32(*flat), f32(*flat), f32(*fine_ctrl.shape)),
        [VMEM, VMEM],
    )(kept(home), kept(ctrl))
    shape = (mem, rows, columns)
    return (ana_h.reshape(shape), ana_u.reshape(shape), ana_v.reshape(shape), fine_out)


def solution(mesh):
    strip = P("member", "region", "fine")
    owner = ("member", "region", "fine")
    fine = P(None, "region", "fine", "member")
    return jax.shard_map(
        shards,
        mesh=mesh,
        in_specs=(
            strip,
            strip,
            strip,
            P("region", "fine"),
            P("region", "fine"),
            P(owner, None, None),
            P(owner, None, None),
            P(owner, None),
            P(owner, None),
            P(owner),
            fine,
        ),
        out_specs=(strip, strip, strip, fine),
        check_vma=False,
    )
```

profile of v0, /device:TPU:0, one launch (start us, length us, event | category | flops | bytes accessed | tf_op | source)
XLA Modules:
  0.0 38.8 jit_solution(8782466896172057151)
XLA Ops:
  0.6 1.2 %shard_map.138 = (f32[264,128]{1,0:T(8,128)S(1)}, f32[264,128]{1,0:T(8,128)S(1)}, f32[2,8,128]{2,1,0:T(8,128)S(1)}, s32[2,8,128]{2,1,0:T(8,128)S(1)}, f32[3,2,1,...) custom-call(f32[128,128]{1,0:T(8,128)} %bitcast.12, ...), custom_call_target="tpu_custom_call" | custom-call | tf_op jit(solution)/shard_map/pallas_call | solution.py:508
  1.8 0.6 %collective-permute-start = (f32[2,8,128]{2,1,0:T(8,128)S(1)}, f32[2,8,128]{2,1,0:T(8,128)S(1)}, u32[]{:S(2)}, u32[]{:S(2)}) collective-permute-start(f32[2,8,128]{2,1,0:T(8,128)S(1)} %get-tuple-element.29), channel_id=1, source_target_pairs={{1,0},{0,1},{3,2},{2,3},{5,4},{4,5},{7,6},{6,7},{9,8},{8,9},{11,10... | collective-permute-start | bytes 24584 | tf_op jit(solution)/shard_map/ppermute | solution.py:31
  2.4 0.9 %shard_map.139 = (f32[2,128,128]{2,1,0:T(8,128)S(1)}, f32[2,128,128]{2,1,0:T(8,128)S(1)}) custom-call(s32[2,8,128]{2,1,0:T(8,128)S(1)} %get-tuple-element.30.live_ref, s32[2,4,512]{2,1,0:T(4,128)S(1)} %get-tuple-element.31.index_ref, f32[2,4,512]{2,1,0:T(4,128)S(1)} %get-tuple-element.32.weight_ref, f32[2,512]{1,0:T(2,128)S(1)} %get-tuple-element.33.value_ref, ...), custom_call_target="tpu_custom_call" | custom-call | flops 201326592 | bytes 1048576 | tf_op jit(solution)/shard_map/pallas_call | solution.py:539
  3.3 0.0 collective-permute-done.west_ref.east_ref
  3.3 0.2 shard_map.140
  3.4 2.8 %collective-permute-start.1 = (f32[152,128]{1,0:T(8,128)S(1)}, f32[152,128]{1,0:T(8,128)S(1)}, u32[]{:S(2)}, u32[]{:S(2)}) collective-permute-start(f32[152,128]{1,0:T(8,128)S(1)} %get-tuple-element.37), channel_id=1, source_target_pairs={{0,2},{2,0},{4,6},{6,4},{1,3},{3,1},{5,7},{7,5},{8,10},{10,8},{12,... | collective-permute-start | bytes 233480 | tf_op jit(solution)/shard_map/ppermute | solution.py:450
  6.2 1.5 %collective-permute-start.2 = (f32[152,128]{1,0:T(8,128)S(1)}, f32[152,128]{1,0:T(8,128)S(1)}, u32[]{:S(2)}, u32[]{:S(2)}) collective-permute-start(f32[152,128]{1,0:T(8,128)S(1)} %get-tuple-element.38), channel_id=1, source_target_pairs={{0,4},{2,6},{4,0},{6,2},{1,5},{3,7},{5,1},{7,3},{8,12},{10,14},{12... | collective-permute-start | bytes 233480 | tf_op jit(solution)/shard_map/ppermute | solution.py:450
  7.8 0.0 collective-permute-start.3
  7.8 1.2 %collective-permute-done.1.refs_1_ = f32[152,128]{1,0:T(8,128)S(1)} collective-permute-done((f32[152,128]{1,0:T(8,128)S(1)}, f32[152,128]{1,0:T(8,128)S(1)}, u32[]{:S(2)}, u32[]{:S(2)}) %collective-permute-start.1) | collective-permute-done | bytes 77856 | tf_op jit(solution)/shard_map/ppermute | solution.py:450
  9.0 2.4 %collective-permute-done.2.refs_2_ = f32[152,128]{1,0:T(8,128)S(1)} collective-permute-done((f32[152,128]{1,0:T(8,128)S(1)}, f32[152,128]{1,0:T(8,128)S(1)}, u32[]{:S(2)}, u32[]{:S(2)}) %collective-permute-start.2) | collective-permute-done | bytes 77856 | tf_op jit(solution)/shard_map/ppermute | solution.py:450
  11.4 1.7 %collective-permute-done.3.refs_3_ = f32[152,128]{1,0:T(8,128)S(1)} collective-permute-done((f32[152,128]{1,0:T(8,128)S(1)}, f32[152,128]{1,0:T(8,128)S(1)}, u32[]{:S(2)}, u32[]{:S(2)}) %collective-permute-start.3) | collective-permute-done | bytes 77856 | tf_op jit(solution)/shard_map/ppermute | solution.py:450
  13.1 0.5 %shard_map.141 = (f32[96,128]{1,0:T(8,128)S(1)}, f32[96,128]{1,0:T(8,128)S(1)}, f32[96,128]{1,0:T(8,128)S(1)}, f32[96,128]{1,0:T(8,128)S(1)}) custom-call(f32[152,128]{1,0:T(8,128)S(1)} %get-tuple-element.36.refs_0_, f32[152,128]{1,0:T(8,128)S(1)} %collective-permute-done.1.refs_1_, f32[152,128]{1,0:T(8,128)S(1)} %collective-permute-done.2.refs_2_, ...), custom_call_target="tpu_custom_call" | custom-call | tf_op jit(solution)/shard_map/pallas_call | solution.py:556
  13.6 1.6 %collective-permute-start.4 = (f32[96,128]{1,0:T(8,128)S(1)}, f32[96,128]{1,0:T(8,128)S(1)}, u32[]{:S(2)}, u32[]{:S(2)}) collective-permute-start(f32[96,128]{1,0:T(8,128)S(1)} %get-tuple-element.41), channel_id=1, source_target_pairs={{0,8},{8,0},{16,24},{24,16},{1,9},{9,1},{17,25},{25,17},{2,10},{10... | collective-permute-start | bytes 147464 | tf_op jit(solution)/shard_map/ppermute | solution.py:450
  15.2 2.6 %collective-permute-start.5 = (f32[96,128]{1,0:T(8,128)S(1)}, f32[96,128]{1,0:T(8,128)S(1)}, u32[]{:S(2)}, u32[]{:S(2)}) collective-permute-start(f32[96,128]{1,0:T(8,128)S(1)} %get-tuple-element.42), channel_id=1, source_target_pairs={{0,16},{8,24},{16,0},{24,8},{1,17},{9,25},{17,1},{25,9},{2,18},{10... | collective-permute-start | bytes 147464 | tf_op jit(solution)/shard_map/ppermute | solution.py:450
  17.8 0.2 collective-permute-start.6
  18.1 0.0 collective-permute-done.4.refs_1_
  18.1 3.2 %collective-permute-done.5.refs_2_ = f32[96,128]{1,0:T(8,128)S(1)} collective-permute-done((f32[96,128]{1,0:T(8,128)S(1)}, f32[96,128]{1,0:T(8,128)S(1)}, u32[]{:S(2)}, u32[]{:S(2)}) %collective-permute-start.5) | collective-permute-done | bytes 49184 | tf_op jit(solution)/shard_map/ppermute | solution.py:450
  21.3 2.4 %collective-permute-done.6.refs_3_ = f32[96,128]{1,0:T(8,128)S(1)} collective-permute-done((f32[96,128]{1,0:T(8,128)S(1)}, f32[96,128]{1,0:T(8,128)S(1)}, u32[]{:S(2)}, u32[]{:S(2)}) %collective-permute-start.6) | collective-permute-done | bytes 49184 | tf_op jit(solution)/shard_map/ppermute | solution.py:450
  23.7 3.4 %shard_map.142 = f32[400,128]{1,0:T(8,128)S(1)} custom-call(f32[96,128]{1,0:T(8,128)S(1)} %get-tuple-element.40.refs_0_, f32[96,128]{1,0:T(8,128)S(1)} %collective-permute-done.4.refs_1_, f32[96,128]{1,0:T(8,128)S(1)} %collective-permute-done.5.refs_2_, f32[96,128]{1,0:T(8,128)S(1)} %collective-permute-done.6.refs_3_, ...), custom_call_target="tpu_custom_call" | custom-call | tf_op jit(solution)/shard_map/pallas_call | solution.py:569
  27.2 10.7 %all_to_all.5 = f32[16,25,1,128]{3,2,1,0:T(1,128)S(1)} all-to-all(f32[16,25,1,128]{3,2,1,0:T(1,128)S(1)} %bitcast.11), channel_id=1, replica_groups=mesh['member'=4,'region'=4,'fine'=2] {'member','region'}, dimensions={0} | all-to-all | bytes 409600 | tf_op jit(solution)/shard_map/all_to_all | solution.py:459
  37.9 0.9 %shard_map.143 = (f32[128,128]{1,0:T(8,128)}, f32[128,128]{1,0:T(8,128)}, f32[128,128]{1,0:T(8,128)}, f32[3,2,1,128]{3,2,1,0:T(1,128)}) custom-call(f32[400,128]{1,0:T(8,128)S(1)} %bitcast.10, f32[3,2,1,128]{3,2,1,0:T(1,128)S(1)} %get-tuple-element.45.ctrl_ref), custom_call_target="tpu_custom_call" | custom-call | tf_op jit(solution)/shard_map/pallas_call | solution.py:593
Async XLA Ops:
  1.8 1.5 %collective-permute-start = (f32[2,8,128]{2,1,0:T(8,128)S(1)}, f32[2,8,128]{2,1,0:T(8,128)S(1)}, u32[]{:S(2)}, u32[]{:S(2)}) collective-permute-start(f32[2,8,128]{2,1,0:T(8,128)S(1)} %get-tuple-element.29), channel_id=1, source_target_pairs={{1,0},{0,1},{3,2},{2,3},{5,4},{4,5},{7,6},{6,7},{9,8},{8,9},{11,10... | collective-permute-start | bytes 24584 | tf_op jit(solution)/shard_map/ppermute | solution.py:31
  3.4 5.6 %collective-permute-start.1 = (f32[152,128]{1,0:T(8,128)S(1)}, f32[152,128]{1,0:T(8,128)S(1)}, u32[]{:S(2)}, u32[]{:S(2)}) collective-permute-start(f32[152,128]{1,0:T(8,128)S(1)} %get-tuple-element.37), channel_id=1, source_target_pairs={{0,2},{2,0},{4,6},{6,4},{1,3},{3,1},{5,7},{7,5},{8,10},{10,8},{12,... | collective-permute-start | bytes 233480 | tf_op jit(solution)/shard_map/ppermute | solution.py:450
  6.2 5.1 %collective-permute-start.2 = (f32[152,128]{1,0:T(8,128)S(1)}, f32[152,128]{1,0:T(8,128)S(1)}, u32[]{:S(2)}, u32[]{:S(2)}) collective-permute-start(f32[152,128]{1,0:T(8,128)S(1)} %get-tuple-element.38), channel_id=1, source_target_pairs={{0,4},{2,6},{4,0},{6,2},{1,5},{3,7},{5,1},{7,3},{8,12},{10,14},{12... | collective-permute-start | bytes 233480 | tf_op jit(solution)/shard_map/ppermute | solution.py:450
  7.8 5.3 %collective-permute-start.3 = (f32[152,128]{1,0:T(8,128)S(1)}, f32[152,128]{1,0:T(8,128)S(1)}, u32[]{:S(2)}, u32[]{:S(2)}) collective-permute-start(f32[152,128]{1,0:T(8,128)S(1)} %get-tuple-element.39), channel_id=1, source_target_pairs={{0,6},{2,4},{4,2},{6,0},{1,7},{3,5},{5,3},{7,1},{8,14},{10,12},{12... | collective-permute-start | bytes 233480 | tf_op jit(solution)/shard_map/ppermute | solution.py:450
  13.6 4.5 %collective-permute-start.4 = (f32[96,128]{1,0:T(8,128)S(1)}, f32[96,128]{1,0:T(8,128)S(1)}, u32[]{:S(2)}, u32[]{:S(2)}) collective-permute-start(f32[96,128]{1,0:T(8,128)S(1)} %get-tuple-element.41), channel_id=1, source_target_pairs={{0,8},{8,0},{16,24},{24,16},{1,9},{9,1},{17,25},{25,17},{2,10},{10... | collective-permute-start | bytes 147464 | tf_op jit(solution)/shard_map/ppermute | solution.py:450
  15.2 6.0 %collective-permute-start.5 = (f32[96,128]{1,0:T(8,128)S(1)}, f32[96,128]{1,0:T(8,128)S(1)}, u32[]{:S(2)}, u32[]{:S(2)}) collective-permute-start(f32[96,128]{1,0:T(8,128)S(1)} %get-tuple-element.42), channel_id=1, source_target_pairs={{0,16},{8,24},{16,0},{24,8},{1,17},{9,25},{17,1},{25,9},{2,18},{10... | collective-permute-start | bytes 147464 | tf_op jit(solution)/shard_map/ppermute | solution.py:450
  17.8 5.9 %collective-permute-start.6 = (f32[96,128]{1,0:T(8,128)S(1)}, f32[96,128]{1,0:T(8,128)S(1)}, u32[]{:S(2)}, u32[]{:S(2)}) collective-permute-start(f32[96,128]{1,0:T(8,128)S(1)} %get-tuple-element.43), channel_id=1, source_target_pairs={{0,24},{8,16},{16,8},{24,0},{1,25},{9,17},{17,9},{25,1},{2,26},{10... | collective-permute-start | bytes 147464 | tf_op jit(solution)/shard_map/ppermute | solution.py:450
where the time goes:
time: 39 us; the launch traced here: 38.8 us
  waiting for transfers between devices  11 us (28%)
  blocking collectives  10.7 us (27%)
  starting transfers between devices  9.35 us (24%)
  Pallas kernels  7.08 us (18%)
  between operations  0.69 us (2%)
    ppermute x6, waiting for transfers between devices, swapped_blocks(): moved.append(lax.ppermute(blocks[s], axis, routes[s]))  11 us
    all_to_all x1, blocking collectives, exchanged(): lax.all_to_all(dense, axes, split_axis=0, concat_axis=0, tiled=True)  10.7 us
    ppermute x6, starting transfers between devices, swapped_blocks(): moved.append(lax.ppermute(blocks[s], axis, routes[s]))  8.79 us
    pallas_call x1, Pallas kernels, shards(): call(functools.partial(region_kernel, *layout), back_shape, [VMEM] * (gro...  3.43 us
    pallas_call x1, Pallas kernels, shards(): call(functools.partial(turn_kernel, mem, len(later)), (near(columns + TIL...  1.17 us
    pallas_call x1, Pallas kernels, shards(): call(functools.partial(home_kernel, mem, strips, width), (f32(*flat), f32...  0.91 us
    pallas_call x1, Pallas kernels, shards(): call(observe_kernel, (near(REG_DEV, padded, padded), near(REG_DEV, padded...  0.89 us
  transfers between devices with their start and end apart: 7, of which 5 were waited for; matrix products, arithmetic and copies ran while one was open for 0% of the time, Pallas kernels for 2%

commit v1 on v0

--- a/solution.py
+++ b/solution.py
@@ -60,8 +60,14 @@
     return jnp.concatenate(split(value), axis=1)
 
 
+def filled(value, rows):
+    if value.shape[0] == rows:
+        return value
+    return jnp.concatenate([value, jnp.zeros((rows - value.shape[0], value.shape[1]), value.dtype)], axis=0)
+
+
 def stacked(value):
-    both = jnp.concatenate(split(value), axis=1)
+    both = filled(jnp.concatenate(split(value), axis=1), value.shape[1])
     return jnp.concatenate([both, both], axis=0)
 
 
@@ -71,12 +77,24 @@
     return out[:, :half] + out[:, half:]
 
 
-def squared(value):
-    both = jnp.concatenate(split(value), axis=0)
-    out = lax.dot_general(both, both, NT, preferred_element_type=jnp.float32)
+def squared(value, columns):
+    high, low = split(value)
+    both = jnp.concatenate([high, low], axis=0)
+    wide = jnp.concatenate([filled(high, columns), filled(low, columns)], axis=0)
+    out = lax.dot_general(both, wide, NT, preferred_element_type=jnp.float32)
+    out = out[:, :columns] + out[:, columns:]
     half = out.shape[0] // 2
-    out = out[:, :half] + out[:, half:]
     return out[:half] + out[half:]
+
+
+def applied_to(left, value):
+    columns = left.shape[1]
+    wide = beside(left)
+    high, low = (filled(part, columns) for part in split(value))
+    dot = functools.partial(
+        lax.dot_general, dimension_numbers=NN, preferred_element_type=jnp.float32
+    )
+    return dot(wide, jnp.concatenate([high, high], axis=0)) + dot(wide[:, :columns], low)
 
 
 BACK_ROWS = 3 * TILE + 1
@@ -213,19 +231,18 @@
 
 
 def collect(got_refs, all_ref, x_ref):
-    states = all_ref.shape[1]
     mine = lax.axis_index("member")
     for s, ref in enumerate(got_refs):
         all_ref[mine ^ s] = ref[...]
     for p in range(len(got_refs) // 2):
         even, odd = all_ref[2 * p], all_ref[2 * p + 1]
         lanes = slice(p * LANES, (p + 1) * LANES)
-        x_ref[0, :states, lanes] = low_pair(even, odd)
-        x_ref[1, :states, lanes] = high_pair(even, odd)
+        x_ref[0, :, lanes] = low_pair(even, odd)
+        x_ref[1, :, lanes] = high_pair(even, odd)
 
 
 def observe_kernel(live_ref, index_ref, weight_ref, value_ref, var_ref, info_ref, pull_ref):
-    states = info_ref.shape[1]
+    states, padded = info_ref.shape[1:]
     obs = index_ref.shape[2]
     for q in range(REG_DEV):
         state = row_of((states, obs))
@@ -237,15 +254,19 @@
         inverse = jnp.where(live, 1.0 / var_ref[q : q + 1, :], 0.0)
         scaled = operator * inverse
         info_ref[q] = lax.dot_general(
-            scaled, operator, NT, precision=HIGHEST, preferred_element_type=jnp.float32
+            scaled,
+            filled(operator, padded),
+            NT,
+            precision=HIGHEST,
+            preferred_element_type=jnp.float32,
         )
         pulled = jnp.sum(scaled * value_ref[q : q + 1, :], axis=1, keepdims=True)
         pull_ref[q] = jnp.broadcast_to(pulled, (states, LANES))
 
 
 def analyse(members, x_ref, info_ref, pull_ref, out_ref):
-    states = x_ref.shape[1]
-    square = (states, states)
+    states, padded = info_ref.shape[1:]
+    square = (states, padded)
     diagonal = row_of(square) == lane_of(square)
     identity = jnp.where(diagonal, 1.0, 0.0)
     regions = range(REG_DEV)
@@ -260,7 +281,7 @@
     x = [x_ref[q] for q in regions]
     means = [jnp.sum(x[q], axis=1, keepdims=True) / members for q in regions]
     spreads = [x[q] - means[q] for q in regions]
-    covs = [squared(spreads[q]) for q in regions]
+    covs = [squared(spreads[q], padded) for q in regions]
     gains = [times(beside(covs[q]), stacked(info_ref[q] * scale)) for q in regions]
     rights = [stacked(gains[q]) for q in regions]
     gains_2 = [times(beside(gains[q]), rights[q]) for q in regions]
@@ -291,27 +312,13 @@
         ]
     increments = []
     for q in regions:
-        high, low = split(spreads[q])
-        wide = beside(inverses[q])
-        moved = lax.dot_general(
-            wide, jnp.concatenate([high, high], axis=0), NN, preferred_element_type=jnp.float32
-        )
-        moved = moved + lax.dot_general(
-            wide[:, :states], low, NN, preferred_element_type=jnp.float32
-        )
+        moved = applied_to(inverses[q], spreads[q])
         twice = applied(inverses[q], as_row(applied(inverses[q], pulls[q])))
         factor = 1.5 * identity - 0.5 * iterates[q]
         twice = applied(factor, as_row(applied(factor, as_row(twice))))
         increment = twice * (inverse_norms[q] * scale)
         increments.append(increment)
-        high, low = split(moved * jnp.sqrt(inverse_norms[q]))
-        wide = beside(factor)
-        moved = lax.dot_general(
-            wide, jnp.concatenate([high, high], axis=0), NN, preferred_element_type=jnp.float32
-        )
-        moved = moved + lax.dot_general(
-            wide[:, :states], low, NN, preferred_element_type=jnp.float32
-        )
+        moved = applied_to(factor, moved * jnp.sqrt(inverse_norms[q]))
         out_ref[q] = moved + (means[q] + increment)
     return increments
 
@@ -343,15 +350,17 @@
 
 def region_kernel(groups, strips, width, *refs):
     got_refs, (info_ref, pull_ref, send_ref, all_ref, x_ref, ana_ref) = refs[:groups], refs[groups:]
-    states = all_ref.shape[1]
-    if states < x_ref.shape[1]:
-        x_ref[:, states:, :] = jnp.zeros_like(x_ref[:, states:, :])
     collect(got_refs, all_ref, x_ref)
     increments = analyse(x_ref.shape[2], x_ref, info_ref, pull_ref, ana_ref)
     pack(groups, strips, width, ana_ref, increments, send_ref)
 
 
-def home_kernel(mem, strips, width, got_ref, ctrl_ref, h_ref, u_ref, v_ref, fine_ref):
+def home_kernel(mem, strips, width, got_ref, ctrl_ref, *refs):
+    targets, (h_ref, u_ref, v_ref, fine_ref, sems) = refs[:4], refs[4:]
+    copies = [
+        pltpu.make_async_copy(source, target, sems.at[i])
+        for i, (source, target) in enumerate(zip((h_ref, u_ref, v_ref, fine_ref), targets))
+    ]
     tiles = got_ref.shape[0] // BACK_ROWS * width // LANES
     per_tile = LANES // width
     for i, out_ref in enumerate((h_ref, u_ref, v_ref)):
@@ -366,6 +375,7 @@
             turned = jnp.concatenate(rows, axis=0).T
             out_ref[pl.ds(t, mem, stride=tiles), :] = turned[:mem]
             out_ref[pl.ds(t + 1, mem, stride=tiles), :] = turned[mem:]
+        copies[i].start()
     mine = lax.axis_index("member") * strips
     per_fine = LANES // (2 * width)
     row = row_of((width, LANES))
@@ -385,6 +395,9 @@
             lanes = slice(t * LANES, (t + 1) * LANES)
             for e in range(2):
                 fine_ref[i, e, :, lanes] = ctrl_ref[i, e, :, lanes] + total
+    copies[3].start()
+    for copy in copies:
+        copy.wait()
 
 
 def collect_kernel(groups, *refs):
@@ -428,13 +441,13 @@
     return mean_state + increment + moved, increment
 
 
-def call(kernel, out_shape, specs, scratch=(), cost=None):
+def call(kernel, out_shape, specs, scratch=(), cost=None, place=VMEM):
     many = isinstance(out_shape, tuple)
     return pl.pallas_call(
         kernel,
         out_shape=out_shape,
         in_specs=specs,
-        out_specs=tuple(VMEM for _ in out_shape) if many else VMEM,
+        out_specs=tuple(place for _ in out_shape) if many else place,
         scratch_shapes=scratch,
         cost_estimate=cost,
         compiler_params=pltpu.CompilerParams(vmem_limit_bytes=GRANT),
@@ -538,7 +551,7 @@
         obs = obs_value.shape[1]
         info, pull = call(
             observe_kernel,
-            (near(REG_DEV, padded, padded), near(REG_DEV, padded, LANES)),
+            (near(REG_DEV, states, padded), near(REG_DEV, states, LANES)),
             [VMEM] * 5,
             cost=pl.CostEstimate(
                 flops=12 * REG_DEV * padded * padded * obs, bytes_accessed=1 << 20, transcendentals=0
@@ -572,8 +585,8 @@
             [VMEM] * (groups + 2),
             scratch=[
                 gathered,
-                pltpu.VMEM((REG_DEV, padded, members), jnp.float32),
-                pltpu.VMEM((REG_DEV, padded, members), jnp.float32),
+                pltpu.VMEM((REG_DEV, states, members), jnp.float32),
+                pltpu.VMEM((REG_DEV, states, members), jnp.float32),
             ],
         )(*got, kept(info), kept(pull))
     else:
@@ -594,6 +607,12 @@
         functools.partial(home_kernel, mem, strips, width),
         (f32(*flat), f32(*flat), f32(*flat), f32(*fine_ctrl.shape)),
         [VMEM, VMEM],
+        scratch=[
+            *[pltpu.VMEM(flat, jnp.float32)] * 3,
+            pltpu.VMEM(fine_ctrl.shape, jnp.float32),
+            pltpu.SemaphoreType.DMA((4,)),
+        ],
+        place=HBM,
     )(kept(home), kept(ctrl))
     shape = (mem, rows, columns)
     return (ana_h.reshape(shape), ana_u.reshape(shape), ana_v.reshape(shape), fine_out)

time: 39 us -> 38.9 us (level)
  transfers between devices with their start and end apart: 7 -> 7, of which waited for: 5 -> 6; matrix products, arithmetic and copies ran while one was open for 0% -> 0% of each run, Pallas kernels for 2% -> 2%
where the time goes in v1:
time: 38.9 us; the launch traced here: 38.7 us
  waiting for transfers between devices  11.1 us (29%)
  blocking collectives  10.7 us (28%)
  starting transfers between devices  9.43 us (24%)
  Pallas kernels  6.75 us (17%)
  between operations  0.68 us (2%)
    ppermute x6, waiting for transfers between devices, swapped_blocks(): moved.append(lax.ppermute(blocks[s], axis, routes[s]))  11 us
    all_to_all x1, blocking collectives, exchanged(): lax.all_to_all(dense, axes, split_axis=0, concat_axis=0, tiled=True)  10.7 us
    ppermute x6, starting transfers between devices, swapped_blocks(): moved.append(lax.ppermute(blocks[s], axis, routes[s]))  8.88 us
    pallas_call x1, Pallas kernels, shards(): call(functools.partial(region_kernel, *layout), back_shape, [VMEM] * (gro...  3.26 us
    pallas_call x1, Pallas kernels, shards(): call(functools.partial(turn_kernel, mem, len(later)), (near(columns + TIL...  1.17 us
    pallas_call x1, Pallas kernels, shards(): call(functools.partial(home_kernel, mem, strips, width), (f32(*flat), f32...  0.94 us
  transfers between devices with their start and end apart: 7, of which 6 were waited for; matrix products, arithmetic and copies ran while one was open for 0% of the time, Pallas kernels for 2%

profile of v1, /device:TPU:0, one launch (start us, length us, event | category | flops | bytes accessed | tf_op | source)
XLA Modules:
  0.0 38.7 jit_solution(11856574851176616832)
XLA Ops:
  0.6 1.2 %shard_map.138 = (f32[264,128]{1,0:T(8,128)S(1)}, f32[264,128]{1,0:T(8,128)S(1)}, f32[2,8,128]{2,1,0:T(8,128)S(1)}, s32[2,8,128]{2,1,0:T(8,128)S(1)}, f32[3,2,1,...) custom-call(f32[128,128]{1,0:T(8,128)} %bitcast.12, ...), custom_call_target="tpu_custom_call" | custom-call | tf_op jit(solution)/shard_map/pallas_call | solution.py:521
  1.8 0.6 %collective-permute-start = (f32[2,8,128]{2,1,0:T(8,128)S(1)}, f32[2,8,128]{2,1,0:T(8,128)S(1)}, u32[]{:S(2)}, u32[]{:S(2)}) collective-permute-start(f32[2,8,128]{2,1,0:T(8,128)S(1)} %get-tuple-element.29), channel_id=1, source_target_pairs={{1,0},{0,1},{3,2},{2,3},{5,4},{4,5},{7,6},{6,7},{9,8},{8,9},{11,10... | collective-permute-start | bytes 24584 | tf_op jit(solution)/shard_map/ppermute | solution.py:31
  2.4 0.7 %shard_map.139 = (f32[2,96,128]{2,1,0:T(8,128)S(1)}, f32[2,96,128]{2,1,0:T(8,128)S(1)}) custom-call(s32[2,8,128]{2,1,0:T(8,128)S(1)} %get-tuple-element.30.live_ref, s32[2,4,512]{2,1,0:T(4,128)S(1)} %get-tuple-element.31.index_ref, f32[2,4,512]{2,1,0:T(4,128)S(1)} %get-tuple-element.32.weight_ref, f32[2,512]{1,0:T(2,128)S(1)} %get-tuple-element.33.value_ref, ...), custom_call_target="tpu_custom_call" | custom-call | flops 201326592 | bytes 1048576 | tf_op jit(solution)/shard_map/pallas_call | solution.py:552
  3.1 0.1 collective-permute-done.west_ref.east_ref
  3.2 0.1 shard_map.140
  3.4 2.9 %collective-permute-start.1 = (f32[152,128]{1,0:T(8,128)S(1)}, f32[152,128]{1,0:T(8,128)S(1)}, u32[]{:S(2)}, u32[]{:S(2)}) collective-permute-start(f32[152,128]{1,0:T(8,128)S(1)} %get-tuple-element.37), channel_id=1, source_target_pairs={{0,2},{2,0},{4,6},{6,4},{1,3},{3,1},{5,7},{7,5},{8,10},{10,8},{12,... | collective-permute-start | bytes 233480 | tf_op jit(solution)/shard_map/ppermute | solution.py:463
  6.2 1.5 %collective-permute-start.2 = (f32[152,128]{1,0:T(8,128)S(1)}, f32[152,128]{1,0:T(8,128)S(1)}, u32[]{:S(2)}, u32[]{:S(2)}) collective-permute-start(f32[152,128]{1,0:T(8,128)S(1)} %get-tuple-element.38), channel_id=1, source_target_pairs={{0,4},{2,6},{4,0},{6,2},{1,5},{3,7},{5,1},{7,3},{8,12},{10,14},{12... | collective-permute-start | bytes 233480 | tf_op jit(solution)/shard_map/ppermute | solution.py:463
  7.8 0.0 collective-permute-start.3
  7.8 1.1 %collective-permute-done.1.refs_1_ = f32[152,128]{1,0:T(8,128)S(1)} collective-permute-done((f32[152,128]{1,0:T(8,128)S(1)}, f32[152,128]{1,0:T(8,128)S(1)}, u32[]{:S(2)}, u32[]{:S(2)}) %collective-permute-start.1) | collective-permute-done | bytes 77856 | tf_op jit(solution)/shard_map/ppermute | solution.py:463
  8.9 2.4 %collective-permute-done.2.refs_2_ = f32[152,128]{1,0:T(8,128)S(1)} collective-permute-done((f32[152,128]{1,0:T(8,128)S(1)}, f32[152,128]{1,0:T(8,128)S(1)}, u32[]{:S(2)}, u32[]{:S(2)}) %collective-permute-start.2) | collective-permute-done | bytes 77856 | tf_op jit(solution)/shard_map/ppermute | solution.py:463
  11.4 1.7 %collective-permute-done.3.refs_3_ = f32[152,128]{1,0:T(8,128)S(1)} collective-permute-done((f32[152,128]{1,0:T(8,128)S(1)}, f32[152,128]{1,0:T(8,128)S(1)}, u32[]{:S(2)}, u32[]{:S(2)}) %collective-permute-start.3) | collective-permute-done | bytes 77856 | tf_op jit(solution)/shard_map/ppermute | solution.py:463
  13.1 0.5 %shard_map.141 = (f32[96,128]{1,0:T(8,128)S(1)}, f32[96,128]{1,0:T(8,128)S(1)}, f32[96,128]{1,0:T(8,128)S(1)}, f32[96,128]{1,0:T(8,128)S(1)}) custom-call(f32[152,128]{1,0:T(8,128)S(1)} %get-tuple-element.36.refs_0_, f32[152,128]{1,0:T(8,128)S(1)} %collective-permute-done.1.refs_1_, f32[152,128]{1,0:T(8,128)S(1)} %collective-permute-done.2.refs_2_, ...), custom_call_target="tpu_custom_call" | custom-call | tf_op jit(solution)/shard_map/pallas_call | solution.py:569
  13.6 1.6 %collective-permute-start.4 = (f32[96,128]{1,0:T(8,128)S(1)}, f32[96,128]{1,0:T(8,128)S(1)}, u32[]{:S(2)}, u32[]{:S(2)}) collective-permute-start(f32[96,128]{1,0:T(8,128)S(1)} %get-tuple-element.41), channel_id=1, source_target_pairs={{0,8},{8,0},{16,24},{24,16},{1,9},{9,1},{17,25},{25,17},{2,10},{10... | collective-permute-start | bytes 147464 | tf_op jit(solution)/shard_map/ppermute | solution.py:463
  15.2 2.6 %collective-permute-start.5 = (f32[96,128]{1,0:T(8,128)S(1)}, f32[96,128]{1,0:T(8,128)S(1)}, u32[]{:S(2)}, u32[]{:S(2)}) collective-permute-start(f32[96,128]{1,0:T(8,128)S(1)} %get-tuple-element.42), channel_id=1, source_target_pairs={{0,16},{8,24},{16,0},{24,8},{1,17},{9,25},{17,1},{25,9},{2,18},{10... | collective-permute-start | bytes 147464 | tf_op jit(solution)/shard_map/ppermute | solution.py:463
  17.8 0.2 collective-permute-start.6
  18.1 0.0 collective-permute-done.4.refs_1_
  18.1 3.2 %collective-permute-done.5.refs_2_ = f32[96,128]{1,0:T(8,128)S(1)} collective-permute-done((f32[96,128]{1,0:T(8,128)S(1)}, f32[96,128]{1,0:T(8,128)S(1)}, u32[]{:S(2)}, u32[]{:S(2)}) %collective-permute-start.5) | collective-permute-done | bytes 49184 | tf_op jit(solution)/shard_map/ppermute | solution.py:463
  21.3 2.4 %collective-permute-done.6.refs_3_ = f32[96,128]{1,0:T(8,128)S(1)} collective-permute-done((f32[96,128]{1,0:T(8,128)S(1)}, f32[96,128]{1,0:T(8,128)S(1)}, u32[]{:S(2)}, u32[]{:S(2)}) %collective-permute-start.6) | collective-permute-done | bytes 49184 | tf_op jit(solution)/shard_map/ppermute | solution.py:463
  23.7 3.3 %shard_map.142 = f32[400,128]{1,0:T(8,128)S(1)} custom-call(f32[96,128]{1,0:T(8,128)S(1)} %get-tuple-element.40.refs_0_, f32[96,128]{1,0:T(8,128)S(1)} %collective-permute-done.4.refs_1_, f32[96,128]{1,0:T(8,128)S(1)} %collective-permute-done.5.refs_2_, f32[96,128]{1,0:T(8,128)S(1)} %collective-permute-done.6.refs_3_, ...), custom_call_target="tpu_custom_call" | custom-call | tf_op jit(solution)/shard_map/pallas_call | solution.py:582
  27.0 10.7 %all_to_all.5 = f32[16,25,1,128]{3,2,1,0:T(1,128)S(1)} all-to-all(f32[16,25,1,128]{3,2,1,0:T(1,128)S(1)} %bitcast.11), channel_id=1, replica_groups=mesh['member'=4,'region'=4,'fine'=2] {'member','region'}, dimensions={0} | all-to-all | bytes 409600 | tf_op jit(solution)/shard_map/all_to_all | solution.py:472
  37.7 0.9 %shard_map.143 = (f32[128,128]{1,0:T(8,128)}, f32[128,128]{1,0:T(8,128)}, f32[128,128]{1,0:T(8,128)}, f32[3,2,1,128]{3,2,1,0:T(1,128)}) custom-call(f32[400,128]{1,0:T(8,128)S(1)} %bitcast.10, f32[3,2,1,128]{3,2,1,0:T(1,128)S(1)} %get-tuple-element.45.ctrl_ref), custom_call_target="tpu_custom_call" | custom-call | tf_op jit(solution)/shard_map/pallas_call | solution.py:606
Async XLA Ops:
  1.8 1.4 %collective-permute-start = (f32[2,8,128]{2,1,0:T(8,128)S(1)}, f32[2,8,128]{2,1,0:T(8,128)S(1)}, u32[]{:S(2)}, u32[]{:S(2)}) collective-permute-start(f32[2,8,128]{2,1,0:T(8,128)S(1)} %get-tuple-element.29), channel_id=1, source_target_pairs={{1,0},{0,1},{3,2},{2,3},{5,4},{4,5},{7,6},{6,7},{9,8},{8,9},{11,10... | collective-permute-start | bytes 24584 | tf_op jit(solution)/shard_map/ppermute | solution.py:31
  3.4 5.6 %collective-permute-start.1 = (f32[152,128]{1,0:T(8,128)S(1)}, f32[152,128]{1,0:T(8,128)S(1)}, u32[]{:S(2)}, u32[]{:S(2)}) collective-permute-start(f32[152,128]{1,0:T(8,128)S(1)} %get-tuple-element.37), channel_id=1, source_target_pairs={{0,2},{2,0},{4,6},{6,4},{1,3},{3,1},{5,7},{7,5},{8,10},{10,8},{12,... | collective-permute-start | bytes 233480 | tf_op jit(solution)/shard_map/ppermute | solution.py:463
  6.2 5.1 %collective-permute-start.2 = (f32[152,128]{1,0:T(8,128)S(1)}, f32[152,128]{1,0:T(8,128)S(1)}, u32[]{:S(2)}, u32[]{:S(2)}) collective-permute-start(f32[152,128]{1,0:T(8,128)S(1)} %get-tuple-element.38), channel_id=1, source_target_pairs={{0,4},{2,6},{4,0},{6,2},{1,5},{3,7},{5,1},{7,3},{8,12},{10,14},{12... | collective-permute-start | bytes 233480 | tf_op jit(solution)/shard_map/ppermute | solution.py:463
  7.8 5.3 %collective-permute-start.3 = (f32[152,128]{1,0:T(8,128)S(1)}, f32[152,128]{1,0:T(8,128)S(1)}, u32[]{:S(2)}, u32[]{:S(2)}) collective-permute-start(f32[152,128]{1,0:T(8,128)S(1)} %get-tuple-element.39), channel_id=1, source_target_pairs={{0,6},{2,4},{4,2},{6,0},{1,7},{3,5},{5,3},{7,1},{8,14},{10,12},{12... | collective-permute-start | bytes 233480 | tf_op jit(solution)/shard_map/ppermute | solution.py:463
  13.6 4.5 %collective-permute-start.4 = (f32[96,128]{1,0:T(8,128)S(1)}, f32[96,128]{1,0:T(8,128)S(1)}, u32[]{:S(2)}, u32[]{:S(2)}) collective-permute-start(f32[96,128]{1,0:T(8,128)S(1)} %get-tuple-element.41), channel_id=1, source_target_pairs={{0,8},{8,0},{16,24},{24,16},{1,9},{9,1},{17,25},{25,17},{2,10},{10... | collective-permute-start | bytes 147464 | tf_op jit(solution)/shard_map/ppermute | solution.py:463
  15.2 6.0 %collective-permute-start.5 = (f32[96,128]{1,0:T(8,128)S(1)}, f32[96,128]{1,0:T(8,128)S(1)}, u32[]{:S(2)}, u32[]{:S(2)}) collective-permute-start(f32[96,128]{1,0:T(8,128)S(1)} %get-tuple-element.42), channel_id=1, source_target_pairs={{0,16},{8,24},{16,0},{24,8},{1,17},{9,25},{17,1},{25,9},{2,18},{10... | collective-permute-start | bytes 147464 | tf_op jit(solution)/shard_map/ppermute | solution.py:463
  17.8 5.9 %collective-permute-start.6 = (f32[96,128]{1,0:T(8,128)S(1)}, f32[96,128]{1,0:T(8,128)S(1)}, u32[]{:S(2)}, u32[]{:S(2)}) collective-permute-start(f32[96,128]{1,0:T(8,128)S(1)} %get-tuple-element.43), channel_id=1, source_target_pairs={{0,24},{8,16},{16,8},{24,0},{1,25},{9,17},{17,9},{25,1},{2,26},{10... | collective-permute-start | bytes 147464 | tf_op jit(solution)/shard_map/ppermute | solution.py:463

commit v2 on v1

--- a/solution.py
+++ b/solution.py
@@ -29,6 +29,12 @@
     count = lax.axis_size(axis)
     route = [((i - distance) % count, i) for i in range(count)]
     return lax.ppermute(block, axis, route)
+
+
+def across(slot, strips, fine):
+    if strips != 4 or slot not in (1, 2):
+        return slot
+    return slot + fine % 2 * (3 - 2 * slot)
 
 
 def lane_of(shape):
@@ -140,13 +146,13 @@
 
 def blocks_kernel(groups, strips, width, pair_ref, single_ref, west_ref, east_ref, *refs):
     send_refs = refs[-strips:]
-    me = lax.axis_index("region")
+    me, fine = lax.axis_index("region"), lax.axis_index("fine")
     shape = (TILE, LANES)
     early = row_of(shape) < STEPS
     part = lane_of(shape) % (HALF // 2)
     span = 3 * TILE
     for s, send_ref in enumerate(send_refs):
-        owner = me ^ s
+        owner = me ^ across(s, strips, fine)
         first, last = early & (owner == 0), ~early & (owner == strips - 1)
         courant = jnp.zeros(shape, jnp.float32)
         for p in range(groups // 2):
@@ -179,9 +185,9 @@
     span = width + 2 * STEPS
     per_region = strips // REG_DEV
     cells = per_region * width
-    me = lax.axis_index("region")
+    me, fine = lax.axis_index("region"), lax.axis_index("fine")
     for s, ref in enumerate(got_refs):
-        got_ref[me ^ s] = ref[...]
+        got_ref[me ^ across(s, strips, fine)] = ref[...]
     low = lane_of((TILE, LANES)) < HALF
     tail = 3 * span * (groups // 2)
     for p in range(groups // 2):
@@ -457,10 +463,16 @@
 def swapped_blocks(blocks, axis):
     count = len(blocks)
     if count <= 4:
-        routes = [[(i, i ^ s) for i in range(count)] for s in range(count)]
+        axes = (axis, "fine")
+        fines = lax.axis_size("fine")
         moved = []
         for s in range(1, count):
-            moved.append(lax.ppermute(blocks[s], axis, routes[s]))
+            route = []
+            for i in range(count):
+                for fine in range(fines):
+                    other = i ^ (across(s, count, fine) if axis == "region" else s)
+                    route.append((i * fines + fine, other * fines + fine))
+            moved.append(lax.ppermute(blocks[s], axes, route))
         return [kept(block) for block in [blocks[0], *moved]]
     order = lax.axis_index(axis) ^ jnp.arange(count)
     moved = lax.all_to_all(jnp.stack(blocks)[order], axis, split_axis=0, concat_axis=0, tiled=True)

time: 38.9 us -> 38.9 us (level)
  no operation moved by 1% of the time
where the time goes in v2:
time: 38.9 us; the launch traced here: 38.7 us
  waiting for transfers between devices  11.1 us (29%)
  blocking collectives  10.7 us (28%)
  starting transfers between devices  9.43 us (24%)
  Pallas kernels  6.74 us (17%)
  between operations  0.68 us (2%)
    ppermute x6, waiting for transfers between devices, swapped_blocks(): moved.append(lax.ppermute(blocks[s], axes, route))  11 us
    all_to_all x1, blocking collectives, exchanged(): lax.all_to_all(dense, axes, split_axis=0, concat_axis=0, tiled=True)  10.7 us
    ppermute x6, starting transfers between devices, swapped_blocks(): moved.append(lax.ppermute(blocks[s], axes, route))  8.88 us
    pallas_call x1, Pallas kernels, shards(): call(functools.partial(region_kernel, *layout), back_shape, [VMEM] * (gro...  3.26 us
    pallas_call x1, Pallas kernels, shards(): call(functools.partial(turn_kernel, mem, len(later)), (near(columns + TIL...  1.17 us
    pallas_call x1, Pallas kernels, shards(): call(functools.partial(home_kernel, mem, strips, width), (f32(*flat), f32...  0.94 us
  transfers between devices with their start and end apart: 7, of which 6 were waited for; matrix products, arithmetic and copies ran while one was open for 0% of the time, Pallas kernels for 2%

profile of v2, /device:TPU:0, one launch (start us, length us, event | category | flops | bytes accessed | tf_op | source)
XLA Modules:
  0.0 38.7 jit_solution(267742915192633674)
XLA Ops:
  0.6 1.2 %shard_map.138 = (f32[264,128]{1,0:T(8,128)S(1)}, f32[264,128]{1,0:T(8,128)S(1)}, f32[2,8,128]{2,1,0:T(8,128)S(1)}, s32[2,8,128]{2,1,0:T(8,128)S(1)}, f32[3,2,1,...) custom-call(f32[128,128]{1,0:T(8,128)} %bitcast.12, ...), custom_call_target="tpu_custom_call" | custom-call | tf_op jit(solution)/shard_map/pallas_call | solution.py:533
  1.8 0.6 %collective-permute-start = (f32[2,8,128]{2,1,0:T(8,128)S(1)}, f32[2,8,128]{2,1,0:T(8,128)S(1)}, u32[]{:S(2)}, u32[]{:S(2)}) collective-permute-start(f32[2,8,128]{2,1,0:T(8,128)S(1)} %get-tuple-element.29), channel_id=1, source_target_pairs={{1,0},{0,1},{3,2},{2,3},{5,4},{4,5},{7,6},{6,7},{9,8},{8,9},{11,10... | collective-permute-start | bytes 24584 | tf_op jit(solution)/shard_map/ppermute | solution.py:31
  2.4 0.7 %shard_map.139 = (f32[2,96,128]{2,1,0:T(8,128)S(1)}, f32[2,96,128]{2,1,0:T(8,128)S(1)}) custom-call(s32[2,8,128]{2,1,0:T(8,128)S(1)} %get-tuple-element.30.live_ref, s32[2,4,512]{2,1,0:T(4,128)S(1)} %get-tuple-element.31.index_ref, f32[2,4,512]{2,1,0:T(4,128)S(1)} %get-tuple-element.32.weight_ref, f32[2,512]{1,0:T(2,128)S(1)} %get-tuple-element.33.value_ref, ...), custom_call_target="tpu_custom_call" | custom-call | flops 201326592 | bytes 1048576 | tf_op jit(solution)/shard_map/pallas_call | solution.py:564
  3.1 0.1 collective-permute-done.west_ref.east_ref
  3.2 0.1 shard_map.140
  3.4 2.9 %collective-permute-start.1 = (f32[152,128]{1,0:T(8,128)S(1)}, f32[152,128]{1,0:T(8,128)S(1)}, u32[]{:S(2)}, u32[]{:S(2)}) collective-permute-start(f32[152,128]{1,0:T(8,128)S(1)} %get-tuple-element.37), channel_id=1, source_target_pairs={{0,2},{1,5},{2,0},{3,7},{4,6},{5,1},{6,4},{7,3},{8,10},{9,13},{10,... | collective-permute-start | bytes 233480 | tf_op jit(solution)/shard_map/ppermute | solution.py:475
  6.2 1.5 %collective-permute-start.2 = (f32[152,128]{1,0:T(8,128)S(1)}, f32[152,128]{1,0:T(8,128)S(1)}, u32[]{:S(2)}, u32[]{:S(2)}) collective-permute-start(f32[152,128]{1,0:T(8,128)S(1)} %get-tuple-element.38), channel_id=1, source_target_pairs={{0,4},{1,3},{2,6},{3,1},{4,0},{5,7},{6,2},{7,5},{8,12},{9,11},{10,... | collective-permute-start | bytes 233480 | tf_op jit(solution)/shard_map/ppermute | solution.py:475
  7.8 0.0 collective-permute-start.3
  7.8 0.8 %collective-permute-done.1.refs_1_ = f32[152,128]{1,0:T(8,128)S(1)} collective-permute-done((f32[152,128]{1,0:T(8,128)S(1)}, f32[152,128]{1,0:T(8,128)S(1)}, u32[]{:S(2)}, u32[]{:S(2)}) %collective-permute-start.1) | collective-permute-done | bytes 77856 | tf_op jit(solution)/shard_map/ppermute | solution.py:475
  8.6 2.8 %collective-permute-done.2.refs_2_ = f32[152,128]{1,0:T(8,128)S(1)} collective-permute-done((f32[152,128]{1,0:T(8,128)S(1)}, f32[152,128]{1,0:T(8,128)S(1)}, u32[]{:S(2)}, u32[]{:S(2)}) %collective-permute-start.2) | collective-permute-done | bytes 77856 | tf_op jit(solution)/shard_map/ppermute | solution.py:475
  11.4 1.7 %collective-permute-done.3.refs_3_ = f32[152,128]{1,0:T(8,128)S(1)} collective-permute-done((f32[152,128]{1,0:T(8,128)S(1)}, f32[152,128]{1,0:T(8,128)S(1)}, u32[]{:S(2)}, u32[]{:S(2)}) %collective-permute-start.3) | collective-permute-done | bytes 77856 | tf_op jit(solution)/shard_map/ppermute | solution.py:475
  13.1 0.5 %shard_map.141 = (f32[96,128]{1,0:T(8,128)S(1)}, f32[96,128]{1,0:T(8,128)S(1)}, f32[96,128]{1,0:T(8,128)S(1)}, f32[96,128]{1,0:T(8,128)S(1)}) custom-call(f32[152,128]{1,0:T(8,128)S(1)} %get-tuple-element.36.refs_0_, f32[152,128]{1,0:T(8,128)S(1)} %collective-permute-done.1.refs_1_, f32[152,128]{1,0:T(8,128)S(1)} %collective-permute-done.2.refs_2_, ...), custom_call_target="tpu_custom_call" | custom-call | tf_op jit(solution)/shard_map/pallas_call | solution.py:581
  13.6 1.6 %collective-permute-start.4 = (f32[96,128]{1,0:T(8,128)S(1)}, f32[96,128]{1,0:T(8,128)S(1)}, u32[]{:S(2)}, u32[]{:S(2)}) collective-permute-start(f32[96,128]{1,0:T(8,128)S(1)} %get-tuple-element.41), channel_id=1, source_target_pairs={{0,8},{1,9},{8,0},{9,1},{16,24},{17,25},{24,16},{25,17},{2,10},{3,... | collective-permute-start | bytes 147464 | tf_op jit(solution)/shard_map/ppermute | solution.py:475
  15.2 2.6 %collective-permute-start.5 = (f32[96,128]{1,0:T(8,128)S(1)}, f32[96,128]{1,0:T(8,128)S(1)}, u32[]{:S(2)}, u32[]{:S(2)}) collective-permute-start(f32[96,128]{1,0:T(8,128)S(1)} %get-tuple-element.42), channel_id=1, source_target_pairs={{0,16},{1,17},{8,24},{9,25},{16,0},{17,1},{24,8},{25,9},{2,18},{3,... | collective-permute-start | bytes 147464 | tf_op jit(solution)/shard_map/ppermute | solution.py:475
  17.8 0.2 collective-permute-start.6
  18.0 0.0 collective-permute-done.4.refs_1_
  18.0 3.2 %collective-permute-done.5.refs_2_ = f32[96,128]{1,0:T(8,128)S(1)} collective-permute-done((f32[96,128]{1,0:T(8,128)S(1)}, f32[96,128]{1,0:T(8,128)S(1)}, u32[]{:S(2)}, u32[]{:S(2)}) %collective-permute-start.5) | collective-permute-done | bytes 49184 | tf_op jit(solution)/shard_map/ppermute | solution.py:475
  21.3 2.4 %collective-permute-done.6.refs_3_ = f32[96,128]{1,0:T(8,128)S(1)} collective-permute-done((f32[96,128]{1,0:T(8,128)S(1)}, f32[96,128]{1,0:T(8,128)S(1)}, u32[]{:S(2)}, u32[]{:S(2)}) %collective-permute-start.6) | collective-permute-done | bytes 49184 | tf_op jit(solution)/shard_map/ppermute | solution.py:475
  23.7 3.3 %shard_map.142 = f32[400,128]{1,0:T(8,128)S(1)} custom-call(f32[96,128]{1,0:T(8,128)S(1)} %get-tuple-element.40.refs_0_, f32[96,128]{1,0:T(8,128)S(1)} %collective-permute-done.4.refs_1_, f32[96,128]{1,0:T(8,128)S(1)} %collective-permute-done.5.refs_2_, f32[96,128]{1,0:T(8,128)S(1)} %collective-permute-done.6.refs_3_, ...), custom_call_target="tpu_custom_call" | custom-call | tf_op jit(solution)/shard_map/pallas_call | solution.py:594
  27.0 10.7 %all_to_all.5 = f32[16,25,1,128]{3,2,1,0:T(1,128)S(1)} all-to-all(f32[16,25,1,128]{3,2,1,0:T(1,128)S(1)} %bitcast.11), channel_id=1, replica_groups=mesh['member'=4,'region'=4,'fine'=2] {'member','region'}, dimensions={0} | all-to-all | bytes 409600 | tf_op jit(solution)/shard_map/all_to_all | solution.py:484
  37.7 0.9 %shard_map.143 = (f32[128,128]{1,0:T(8,128)}, f32[128,128]{1,0:T(8,128)}, f32[128,128]{1,0:T(8,128)}, f32[3,2,1,128]{3,2,1,0:T(1,128)}) custom-call(f32[400,128]{1,0:T(8,128)S(1)} %bitcast.10, f32[3,2,1,128]{3,2,1,0:T(1,128)S(1)} %get-tuple-element.45.ctrl_ref), custom_call_target="tpu_custom_call" | custom-call | tf_op jit(solution)/shard_map/pallas_call | solution.py:618
Async XLA Ops:
  1.8 1.4 %collective-permute-start = (f32[2,8,128]{2,1,0:T(8,128)S(1)}, f32[2,8,128]{2,1,0:T(8,128)S(1)}, u32[]{:S(2)}, u32[]{:S(2)}) collective-permute-start(f32[2,8,128]{2,1,0:T(8,128)S(1)} %get-tuple-element.29), channel_id=1, source_target_pairs={{1,0},{0,1},{3,2},{2,3},{5,4},{4,5},{7,6},{6,7},{9,8},{8,9},{11,10... | collective-permute-start | bytes 24584 | tf_op jit(solution)/shard_map/ppermute | solution.py:31
  3.4 5.3 %collective-permute-start.1 = (f32[152,128]{1,0:T(8,128)S(1)}, f32[152,128]{1,0:T(8,128)S(1)}, u32[]{:S(2)}, u32[]{:S(2)}) collective-permute-start(f32[152,128]{1,0:T(8,128)S(1)} %get-tuple-element.37), channel_id=1, source_target_pairs={{0,2},{1,5},{2,0},{3,7},{4,6},{5,1},{6,4},{7,3},{8,10},{9,13},{10,... | collective-permute-start | bytes 233480 | tf_op jit(solution)/shard_map/ppermute | solution.py:475
  6.2 5.1 %collective-permute-start.2 = (f32[152,128]{1,0:T(8,128)S(1)}, f32[152,128]{1,0:T(8,128)S(1)}, u32[]{:S(2)}, u32[]{:S(2)}) collective-permute-start(f32[152,128]{1,0:T(8,128)S(1)} %get-tuple-element.38), channel_id=1, source_target_pairs={{0,4},{1,3},{2,6},{3,1},{4,0},{5,7},{6,2},{7,5},{8,12},{9,11},{10,... | collective-permute-start | bytes 233480 | tf_op jit(solution)/shard_map/ppermute | solution.py:475
  7.8 5.3 %collective-permute-start.3 = (f32[152,128]{1,0:T(8,128)S(1)}, f32[152,128]{1,0:T(8,128)S(1)}, u32[]{:S(2)}, u32[]{:S(2)}) collective-permute-start(f32[152,128]{1,0:T(8,128)S(1)} %get-tuple-element.39), channel_id=1, source_target_pairs={{0,6},{1,7},{2,4},{3,5},{4,2},{5,3},{6,0},{7,1},{8,14},{9,15},{10,... | collective-permute-start | bytes 233480 | tf_op jit(solution)/shard_map/ppermute | solution.py:475
  13.6 4.5 %collective-permute-start.4 = (f32[96,128]{1,0:T(8,128)S(1)}, f32[96,128]{1,0:T(8,128)S(1)}, u32[]{:S(2)}, u32[]{:S(2)}) collective-permute-start(f32[96,128]{1,0:T(8,128)S(1)} %get-tuple-element.41), channel_id=1, source_target_pairs={{0,8},{1,9},{8,0},{9,1},{16,24},{17,25},{24,16},{25,17},{2,10},{3,... | collective-permute-start | bytes 147464 | tf_op jit(solution)/shard_map/ppermute | solution.py:475
  15.2 6.0 %collective-permute-start.5 = (f32[96,128]{1,0:T(8,128)S(1)}, f32[96,128]{1,0:T(8,128)S(1)}, u32[]{:S(2)}, u32[]{:S(2)}) collective-permute-start(f32[96,128]{1,0:T(8,128)S(1)} %get-tuple-element.42), channel_id=1, source_target_pairs={{0,16},{1,17},{8,24},{9,25},{16,0},{17,1},{24,8},{25,9},{2,18},{3,... | collective-permute-start | bytes 147464 | tf_op jit(solution)/shard_map/ppermute | solution.py:475
  17.8 5.9 %collective-permute-start.6 = (f32[96,128]{1,0:T(8,128)S(1)}, f32[96,128]{1,0:T(8,128)S(1)}, u32[]{:S(2)}, u32[]{:S(2)}) collective-permute-start(f32[96,128]{1,0:T(8,128)S(1)} %get-tuple-element.43), channel_id=1, source_target_pairs={{0,24},{1,25},{8,16},{9,17},{16,8},{17,9},{24,0},{25,1},{2,26},{3,... | collective-permute-start | bytes 147464 | tf_op jit(solution)/shard_map/ppermute | solution.py:475

commit v3 on v1

--- a/solution.py
+++ b/solution.py
@@ -194,13 +194,7 @@
             parts = []
             for j in range(3):
                 even, odd = first + 6 * p + j, first + 6 * p + 3 + j
-                parts.append(
-                    jnp.where(
-                        low,
-                        jnp.broadcast_to(mixed[:, even : even + 1], (TILE, LANES)),
-                        jnp.broadcast_to(mixed[:, odd : odd + 1], (TILE, LANES)),
-                    )
-                )
+                parts.append(jnp.take_along_axis(mixed, jnp.where(low, even, odd), axis=1))
             return jnp.concatenate(parts, axis=0)
 
         h = [field(r, 0) for r in range(strips)]
@@ -230,6 +224,17 @@
         ref[...] = turned_ref[mine ^ s]
 
 
+def regions_of(even, odd):
+    return [low_pair(even, odd), high_pair(even, odd)]
+
+
+def early_kernel(even_ref, odd_ref, shift_ref, cov_ref):
+    for q, tile in enumerate(regions_of(even_ref[...], odd_ref[...])):
+        shift = jnp.sum(tile, axis=1, keepdims=True) / LANES
+        shift_ref[q] = jnp.broadcast_to(shift, shift_ref.shape[1:])
+        cov_ref[q] = squared(tile - shift, cov_ref.shape[2])
+
+
 def collect(got_refs, all_ref, x_ref):
     mine = lax.axis_index("member")
     for s, ref in enumerate(got_refs):
@@ -237,8 +242,8 @@
     for p in range(len(got_refs) // 2):
         even, odd = all_ref[2 * p], all_ref[2 * p + 1]
         lanes = slice(p * LANES, (p + 1) * LANES)
-        x_ref[0, :, lanes] = low_pair(even, odd)
-        x_ref[1, :, lanes] = high_pair(even, odd)
+        for q, tile in enumerate(regions_of(even, odd)):
+            x_ref[q, :, lanes] = tile
 
 
 def observe_kernel(live_ref, index_ref, weight_ref, value_ref, var_ref, info_ref, pull_ref):
@@ -264,7 +269,7 @@
         pull_ref[q] = jnp.broadcast_to(pulled, (states, LANES))
 
 
-def analyse(members, x_ref, info_ref, pull_ref, out_ref):
+def analyse(members, rest, fill, x_ref, shift_ref, cov_ref, info_ref, pull_ref, out_ref):
     states, padded = info_ref.shape[1:]
     square = (states, padded)
     diagonal = row_of(square) == lane_of(square)
@@ -278,13 +283,16 @@
     def applied(matrix, row):
         return jnp.sum(matrix * row, axis=1, keepdims=True)
 
-    x = [x_ref[q] for q in regions]
-    means = [jnp.sum(x[q], axis=1, keepdims=True) / members for q in regions]
-    spreads = [x[q] - means[q] for q in regions]
-    covs = [squared(spreads[q], padded) for q in regions]
+    shifts = [shift_ref[q][:, 0:1] for q in regions]
+    later = [rest[q] - shifts[q] for q in regions]
+    covs = [cov_ref[q] + squared(later[q], padded) for q in regions]
+    moves = [jnp.sum(later[q], axis=1, keepdims=True) / members for q in regions]
+    covs = [covs[q] - members * (moves[q] * as_row(moves[q])) for q in regions]
+    means = [shifts[q] + moves[q] for q in regions]
     gains = [times(beside(covs[q]), stacked(info_ref[q] * scale)) for q in regions]
     rights = [stacked(gains[q]) for q in regions]
     gains_2 = [times(beside(gains[q]), rights[q]) for q in regions]
+    fill()
     pulls, inverse_norms, iterates, inverses = [], [], [], []
     for q in regions:
         pulled = pull_ref[q][:, 0:1] - applied(info_ref[q], as_row(means[q]))
@@ -300,19 +308,17 @@
         iterates.append(2.25 * first - 1.5 * second + 0.25 * third)
     for _ in range(1, NEWTON - 1):
         rights = [stacked(iterates[q]) for q in regions]
-        lefts = [
-            jnp.concatenate([beside(iterates[q]), beside(inverses[q])], axis=0) for q in regions
+        seconds = [times(beside(iterates[q]), rights[q]) for q in regions]
+        inverses = [
+            1.5 * inverses[q] - 0.5 * times(beside(inverses[q]), rights[q]) for q in regions
         ]
-        both = [times(lefts[q], rights[q]) for q in regions]
-        seconds = [both[q][:states] for q in regions]
         thirds = [times(beside(seconds[q]), rights[q]) for q in regions]
-        inverses = [1.5 * inverses[q] - 0.5 * both[q][states:] for q in regions]
         iterates = [
             2.25 * iterates[q] - 1.5 * seconds[q] + 0.25 * thirds[q] for q in regions
         ]
     increments = []
     for q in regions:
-        moved = applied_to(inverses[q], spreads[q])
+        moved = applied_to(inverses[q], x_ref[q] - means[q])
         twice = applied(inverses[q], as_row(applied(inverses[q], pulls[q])))
         factor = 1.5 * identity - 0.5 * iterates[q]
         twice = applied(factor, as_row(applied(factor, as_row(twice))))
@@ -349,9 +355,16 @@
 
 
 def region_kernel(groups, strips, width, *refs):
-    got_refs, (info_ref, pull_ref, send_ref, all_ref, x_ref, ana_ref) = refs[:groups], refs[groups:]
-    collect(got_refs, all_ref, x_ref)
-    increments = analyse(x_ref.shape[2], x_ref, info_ref, pull_ref, ana_ref)
+    got_refs, refs = refs[:groups], refs[groups:]
+    shift_ref, cov_ref, info_ref, pull_ref, send_ref, all_ref, x_ref, ana_ref = refs
+    pairs = [
+        regions_of(got_refs[s][...], got_refs[s - 1][...]) for s in range(groups - 2, 0, -2)
+    ]
+    rest = [jnp.concatenate([pair[q] for pair in pairs], axis=1) for q in range(REG_DEV)]
+    fill = functools.partial(collect, got_refs, all_ref, x_ref)
+    increments = analyse(
+        x_ref.shape[2], rest, fill, x_ref, shift_ref, cov_ref, info_ref, pull_ref, ana_ref
+    )
     pack(groups, strips, width, ana_ref, increments, send_ref)
 
 
@@ -514,7 +527,7 @@
     assert 3 * groups <= HALF // 2
     flat = (mem * columns // LANES, LANES)
     states = 3 * width * strips // REG_DEV
-    small = states <= members
+    small = states <= members and groups > 2
     later = [fine_ctrl]
     if small:
         later += [obs_index.transpose(0, 2, 1), obs_weight.transpose(0, 2, 1), obs_value, obs_var]
@@ -579,16 +592,24 @@
     back_shape = near(count * BACK_ROWS, LANES)
     gathered = pltpu.VMEM((groups, states, LANES), jnp.float32)
     if small:
+        shift, cov = call(
+            early_kernel,
+            (near(REG_DEV, states, LANES), near(REG_DEV, states, padded)),
+            [VMEM] * 2,
+            cost=pl.CostEstimate(
+                flops=8 * REG_DEV * padded * padded * LANES, bytes_accessed=1 << 18, transcendentals=0
+            ),
+        )(got[0], got[-1])
         back = call(
             functools.partial(region_kernel, *layout),
             back_shape,
-            [VMEM] * (groups + 2),
+            [VMEM] * (groups + 4),
             scratch=[
                 gathered,
                 pltpu.VMEM((REG_DEV, states, members), jnp.float32),
                 pltpu.VMEM((REG_DEV, states, members), jnp.float32),
             ],
-        )(*got, kept(info), kept(pull))
+        )(*got, kept(shift), kept(cov), kept(info), kept(pull))
     else:
         x = call(
             functools.partial(collect_kernel, groups),

time: 38.9 us -> 38 us (0.977)
  waiting for transfers between devices: 11.1 us -> 9.21 us
  blocking collectives: 10.7 us -> 11.6 us
    ppermute x6, waiting for transfers between devices: 11 us -> 9.09 us  [swapped_blocks(): moved.append(lax.ppermute(blocks[s], axis, routes[s]))]
    all_to_all x1, blocking collectives: 10.7 us -> 11.6 us  [exchanged(): lax.all_to_all(dense, axes, split_axis=0, concat_axis=0, tiled=True)]
    pallas_call x0 -> x1, Pallas kernels: none -> 0.39 us  [shards(): call(early_kernel, (near(REG_DEV, states, LANES), near(REG_DEV, states, p...]
  transfers between devices with their start and end apart: 7 -> 7, of which waited for: 6 -> 7; matrix products, arithmetic and copies ran while one was open for 0% -> 0% of each run, Pallas kernels for 2% -> 3%
where the time goes in v3:
time: 38 us; the launch traced here: 37.8 us
  blocking collectives  11.6 us (31%)
  starting transfers between devices  9.44 us (25%)
  waiting for transfers between devices  9.21 us (24%)
  Pallas kernels  6.92 us (18%)
  between operations  0.69 us (2%)
    all_to_all x1, blocking collectives, exchanged(): lax.all_to_all(dense, axes, split_axis=0, concat_axis=0, tiled=True)  11.6 us
    ppermute x6, waiting for transfers between devices, swapped_blocks(): moved.append(lax.ppermute(blocks[s], axis, routes[s]))  9.09 us
    ppermute x6, starting transfers between devices, swapped_blocks(): moved.append(lax.ppermute(blocks[s], axis, routes[s]))  8.88 us
    pallas_call x1, Pallas kernels, shards(): call(functools.partial(region_kernel, *layout), back_shape, [VMEM] * (gro...  3.13 us
    pallas_call x1, Pallas kernels, shards(): call(functools.partial(turn_kernel, mem, len(later)), (near(columns + TIL...  1.17 us
    pallas_call x1, Pallas kernels, shards(): call(functools.partial(home_kernel, mem, strips, width), (f32(*flat), f32...  0.94 us
  transfers between devices with their start and end apart: 7, of which 7 were waited for; matrix products, arithmetic and copies ran while one was open for 0% of the time, Pallas kernels for 3%

profile of v3, /device:TPU:0, one launch (start us, length us, event | category | flops | bytes accessed | tf_op | source)
XLA Modules:
  0.0 37.8 jit_solution(1237270520645956027)
XLA Ops:
  0.6 1.2 %shard_map.138 = (f32[264,128]{1,0:T(8,128)S(1)}, f32[264,128]{1,0:T(8,128)S(1)}, f32[2,8,128]{2,1,0:T(8,128)S(1)}, s32[2,8,128]{2,1,0:T(8,128)S(1)}, f32[3,2,1,...) custom-call(f32[128,128]{1,0:T(8,128)} %bitcast.12, ...), custom_call_target="tpu_custom_call" | custom-call | tf_op jit(solution)/shard_map/pallas_call | solution.py:534
  1.8 0.6 %collective-permute-start = (f32[2,8,128]{2,1,0:T(8,128)S(1)}, f32[2,8,128]{2,1,0:T(8,128)S(1)}, u32[]{:S(2)}, u32[]{:S(2)}) collective-permute-start(f32[2,8,128]{2,1,0:T(8,128)S(1)} %get-tuple-element.31), channel_id=1, source_target_pairs={{1,0},{0,1},{3,2},{2,3},{5,4},{4,5},{7,6},{6,7},{9,8},{8,9},{11,10... | collective-permute-start | bytes 24584 | tf_op jit(solution)/shard_map/ppermute | solution.py:31
  2.4 0.7 %shard_map.139 = (f32[2,96,128]{2,1,0:T(8,128)S(1)}, f32[2,96,128]{2,1,0:T(8,128)S(1)}) custom-call(s32[2,8,128]{2,1,0:T(8,128)S(1)} %get-tuple-element.32.live_ref, s32[2,4,512]{2,1,0:T(4,128)S(1)} %get-tuple-element.33.index_ref, f32[2,4,512]{2,1,0:T(4,128)S(1)} %get-tuple-element.34.weight_ref, f32[2,512]{1,0:T(2,128)S(1)} %get-tuple-element.35.value_ref, ...), custom_call_target="tpu_custom_call" | custom-call | flops 201326592 | bytes 1048576 | tf_op jit(solution)/shard_map/pallas_call | solution.py:565
  3.1 0.1 collective-permute-done.west_ref.east_ref
  3.2 0.1 shard_map.140
  3.4 2.9 %collective-permute-start.1 = (f32[152,128]{1,0:T(8,128)S(1)}, f32[152,128]{1,0:T(8,128)S(1)}, u32[]{:S(2)}, u32[]{:S(2)}) collective-permute-start(f32[152,128]{1,0:T(8,128)S(1)} %get-tuple-element.39), channel_id=1, source_target_pairs={{0,2},{2,0},{4,6},{6,4},{1,3},{3,1},{5,7},{7,5},{8,10},{10,8},{12,... | collective-permute-start | bytes 233480 | tf_op jit(solution)/shard_map/ppermute | solution.py:476
  6.2 1.5 %collective-permute-start.2 = (f32[152,128]{1,0:T(8,128)S(1)}, f32[152,128]{1,0:T(8,128)S(1)}, u32[]{:S(2)}, u32[]{:S(2)}) collective-permute-start(f32[152,128]{1,0:T(8,128)S(1)} %get-tuple-element.40), channel_id=1, source_target_pairs={{0,4},{2,6},{4,0},{6,2},{1,5},{3,7},{5,1},{7,3},{8,12},{10,14},{12... | collective-permute-start | bytes 233480 | tf_op jit(solution)/shard_map/ppermute | solution.py:476
  7.8 0.0 collective-permute-start.3
  7.8 1.1 %collective-permute-done.1.refs_1_ = f32[152,128]{1,0:T(8,128)S(1)} collective-permute-done((f32[152,128]{1,0:T(8,128)S(1)}, f32[152,128]{1,0:T(8,128)S(1)}, u32[]{:S(2)}, u32[]{:S(2)}) %collective-permute-start.1) | collective-permute-done | bytes 77856 | tf_op jit(solution)/shard_map/ppermute | solution.py:476
  8.9 2.4 %collective-permute-done.2.refs_2_ = f32[152,128]{1,0:T(8,128)S(1)} collective-permute-done((f32[152,128]{1,0:T(8,128)S(1)}, f32[152,128]{1,0:T(8,128)S(1)}, u32[]{:S(2)}, u32[]{:S(2)}) %collective-permute-start.2) | collective-permute-done | bytes 77856 | tf_op jit(solution)/shard_map/ppermute | solution.py:476
  11.4 1.7 %collective-permute-done.3.refs_3_ = f32[152,128]{1,0:T(8,128)S(1)} collective-permute-done((f32[152,128]{1,0:T(8,128)S(1)}, f32[152,128]{1,0:T(8,128)S(1)}, u32[]{:S(2)}, u32[]{:S(2)}) %collective-permute-start.3) | collective-permute-done | bytes 77856 | tf_op jit(solution)/shard_map/ppermute | solution.py:476
  13.1 0.4 %shard_map.141 = (f32[96,128]{1,0:T(8,128)S(1)}, f32[96,128]{1,0:T(8,128)S(1)}, f32[96,128]{1,0:T(8,128)S(1)}, f32[96,128]{1,0:T(8,128)S(1)}) custom-call(f32[152,128]{1,0:T(8,128)S(1)} %get-tuple-element.38.refs_0_, f32[152,128]{1,0:T(8,128)S(1)} %collective-permute-done.1.refs_1_, f32[152,128]{1,0:T(8,128)S(1)} %collective-permute-done.2.refs_2_, ...), custom_call_target="tpu_custom_call" | custom-call | tf_op jit(solution)/shard_map/pallas_call | solution.py:582
  13.5 3.7 %collective-permute-start.6 = (f32[96,128]{1,0:T(8,128)S(1)}, f32[96,128]{1,0:T(8,128)S(1)}, u32[]{:S(2)}, u32[]{:S(2)}) collective-permute-start(f32[96,128]{1,0:T(8,128)S(1)} %get-tuple-element.45), channel_id=1, source_target_pairs={{0,24},{8,16},{16,8},{24,0},{1,25},{9,17},{17,9},{25,1},{2,26},{10... | collective-permute-start | bytes 147464 | tf_op jit(solution)/shard_map/ppermute | solution.py:476
  17.2 0.0 collective-permute-start.4
  17.2 0.8 %collective-permute-start.5 = (f32[96,128]{1,0:T(8,128)S(1)}, f32[96,128]{1,0:T(8,128)S(1)}, u32[]{:S(2)}, u32[]{:S(2)}) collective-permute-start(f32[96,128]{1,0:T(8,128)S(1)} %get-tuple-element.44), channel_id=1, source_target_pairs={{0,16},{8,24},{16,0},{24,8},{1,17},{9,25},{17,1},{25,9},{2,18},{10... | collective-permute-start | bytes 147464 | tf_op jit(solution)/shard_map/ppermute | solution.py:476
  18.0 1.6 %collective-permute-done.6.odd_ref.refs_3_ = f32[96,128]{1,0:T(8,128)S(1)} collective-permute-done((f32[96,128]{1,0:T(8,128)S(1)}, f32[96,128]{1,0:T(8,128)S(1)}, u32[]{:S(2)}, u32[]{:S(2)}) %collective-permute-start.6) | collective-permute-done | bytes 49184 | tf_op jit(solution)/shard_map/ppermute | solution.py:476
  19.6 0.4 %shard_map.142 = (f32[2,96,128]{2,1,0:T(8,128)S(1)}, f32[2,96,128]{2,1,0:T(8,128)S(1)}) custom-call(f32[96,128]{1,0:T(8,128)S(1)} %get-tuple-element.42.even_ref.refs_0_, f32[96,128]{1,0:T(8,128)S(1)} %collective-permute-done.6.odd_ref.refs_3_), custom_call_target="tpu_custom_call" | custom-call | flops 33554432 | bytes 262144 | tf_op jit(solution)/shard_map/pallas_call | solution.py:595
  20.0 1.3 %collective-permute-done.4.refs_1_ = f32[96,128]{1,0:T(8,128)S(1)} collective-permute-done((f32[96,128]{1,0:T(8,128)S(1)}, f32[96,128]{1,0:T(8,128)S(1)}, u32[]{:S(2)}, u32[]{:S(2)}) %collective-permute-start.4) | collective-permute-done | bytes 49184 | tf_op jit(solution)/shard_map/ppermute | solution.py:476
  21.3 0.9 %collective-permute-done.5.refs_2_ = f32[96,128]{1,0:T(8,128)S(1)} collective-permute-done((f32[96,128]{1,0:T(8,128)S(1)}, f32[96,128]{1,0:T(8,128)S(1)}, u32[]{:S(2)}, u32[]{:S(2)}) %collective-permute-start.5) | collective-permute-done | bytes 49184 | tf_op jit(solution)/shard_map/ppermute | solution.py:476
  22.2 3.1 %shard_map.143 = f32[400,128]{1,0:T(8,128)S(1)} custom-call(f32[96,128]{1,0:T(8,128)S(1)} %get-tuple-element.42.even_ref.refs_0_, f32[96,128]{1,0:T(8,128)S(1)} %collective-permute-done.4.refs_1_, f32[96,128]{1,0:T(8,128)S(1)} %collective-permute-done.5.refs_2_, f32[96,128]{1,0:T(8,128)S(1)} %collective-permute-done.6.odd_ref.refs_3_, ...), custom_call_target="tpu_custom_call" | custom-call | tf_op jit(solution)/shard_map/pallas_call | solution.py:603
  25.3 11.6 %all_to_all.5 = f32[16,25,1,128]{3,2,1,0:T(1,128)S(1)} all-to-all(f32[16,25,1,128]{3,2,1,0:T(1,128)S(1)} %bitcast.10), channel_id=1, replica_groups=mesh['member'=4,'region'=4,'fine'=2] {'member','region'}, dimensions={0} | all-to-all | bytes 409600 | tf_op jit(solution)/shard_map/all_to_all | solution.py:485
  36.9 0.9 %shard_map.144 = (f32[128,128]{1,0:T(8,128)}, f32[128,128]{1,0:T(8,128)}, f32[128,128]{1,0:T(8,128)}, f32[3,2,1,128]{3,2,1,0:T(1,128)}) custom-call(f32[400,128]{1,0:T(8,128)S(1)} %bitcast.11, f32[3,2,1,128]{3,2,1,0:T(1,128)S(1)} %get-tuple-element.49.ctrl_ref), custom_call_target="tpu_custom_call" | custom-call | tf_op jit(solution)/shard_map/pallas_call | solution.py:627
Async XLA Ops:
  1.8 1.4 %collective-permute-start = (f32[2,8,128]{2,1,0:T(8,128)S(1)}, f32[2,8,128]{2,1,0:T(8,128)S(1)}, u32[]{:S(2)}, u32[]{:S(2)}) collective-permute-start(f32[2,8,128]{2,1,0:T(8,128)S(1)} %get-tuple-element.31), channel_id=1, source_target_pairs={{1,0},{0,1},{3,2},{2,3},{5,4},{4,5},{7,6},{6,7},{9,8},{8,9},{11,10... | collective-permute-start | bytes 24584 | tf_op jit(solution)/shard_map/ppermute | solution.py:31
  3.4 5.6 %collective-permute-start.1 = (f32[152,128]{1,0:T(8,128)S(1)}, f32[152,128]{1,0:T(8,128)S(1)}, u32[]{:S(2)}, u32[]{:S(2)}) collective-permute-start(f32[152,128]{1,0:T(8,128)S(1)} %get-tuple-element.39), channel_id=1, source_target_pairs={{0,2},{2,0},{4,6},{6,4},{1,3},{3,1},{5,7},{7,5},{8,10},{10,8},{12,... | collective-permute-start | bytes 233480 | tf_op jit(solution)/shard_map/ppermute | solution.py:476
  6.2 5.1 %collective-permute-start.2 = (f32[152,128]{1,0:T(8,128)S(1)}, f32[152,128]{1,0:T(8,128)S(1)}, u32[]{:S(2)}, u32[]{:S(2)}) collective-permute-start(f32[152,128]{1,0:T(8,128)S(1)} %get-tuple-element.40), channel_id=1, source_target_pairs={{0,4},{2,6},{4,0},{6,2},{1,5},{3,7},{5,1},{7,3},{8,12},{10,14},{12... | collective-permute-start | bytes 233480 | tf_op jit(solution)/shard_map/ppermute | solution.py:476
  7.8 5.3 %collective-permute-start.3 = (f32[152,128]{1,0:T(8,128)S(1)}, f32[152,128]{1,0:T(8,128)S(1)}, u32[]{:S(2)}, u32[]{:S(2)}) collective-permute-start(f32[152,128]{1,0:T(8,128)S(1)} %get-tuple-element.41), channel_id=1, source_target_pairs={{0,6},{2,4},{4,2},{6,0},{1,7},{3,5},{5,3},{7,1},{8,14},{10,12},{12... | collective-permute-start | bytes 233480 | tf_op jit(solution)/shard_map/ppermute | solution.py:476
  13.5 6.1 %collective-permute-start.6 = (f32[96,128]{1,0:T(8,128)S(1)}, f32[96,128]{1,0:T(8,128)S(1)}, u32[]{:S(2)}, u32[]{:S(2)}) collective-permute-start(f32[96,128]{1,0:T(8,128)S(1)} %get-tuple-element.45), channel_id=1, source_target_pairs={{0,24},{8,16},{16,8},{24,0},{1,25},{9,17},{17,9},{25,1},{2,26},{10... | collective-permute-start | bytes 147464 | tf_op jit(solution)/shard_map/ppermute | solution.py:476
  17.2 4.1 %collective-permute-start.4 = (f32[96,128]{1,0:T(8,128)S(1)}, f32[96,128]{1,0:T(8,128)S(1)}, u32[]{:S(2)}, u32[]{:S(2)}) collective-permute-start(f32[96,128]{1,0:T(8,128)S(1)} %get-tuple-element.43), channel_id=1, source_target_pairs={{0,8},{8,0},{16,24},{24,16},{1,9},{9,1},{17,25},{25,17},{2,10},{10... | collective-permute-start | bytes 147464 | tf_op jit(solution)/shard_map/ppermute | solution.py:476
  17.2 5.0 %collective-permute-start.5 = (f32[96,128]{1,0:T(8,128)S(1)}, f32[96,128]{1,0:T(8,128)S(1)}, u32[]{:S(2)}, u32[]{:S(2)}) collective-permute-start(f32[96,128]{1,0:T(8,128)S(1)} %get-tuple-element.44), channel_id=1, source_target_pairs={{0,16},{8,24},{16,0},{24,8},{1,17},{9,25},{17,1},{25,9},{2,18},{10... | collective-permute-start | bytes 147464 | tf_op jit(solution)/shard_map/ppermute | solution.py:476

commit v4 on v3

--- a/solution.py
+++ b/solution.py
@@ -100,25 +100,48 @@
 BACK_ROWS = 3 * TILE + 1
 
 
-def turn_kernel(mem, later, *refs):
-    sources, refs = refs[: 6 + later], refs[6 + later :]
-    pair_ref, single_ref, edge_ref, live_ref = refs[:4]
-    targets, sems = refs[4 + later : -1] + refs[4 : 4 + later], refs[-1]
+def edge_kernel(mem, *refs):
+    sources, edge_ref, targets, sems = refs[:5], refs[5], refs[6:-1], refs[-1]
     copies = [
         pltpu.make_async_copy(source, target, sems.at[i])
         for i, (source, target) in enumerate(zip(sources, targets))
     ]
     for copy in copies:
         copy.start()
-    h_ref, u_ref, v_ref, zonal_ref, merid_ref, count_ref = targets[:6]
+    for copy in copies:
+        copy.wait()
+    fields, courants = targets[:3], targets[3:]
+    tiles = fields[0].shape[0] // mem
+    end = (tiles - 1) * LANES
+
+    def outermost(first, last):
+        return jnp.where(lane_of(first.shape) < HALF, first, last)
+
+    h, u, v = (
+        outermost(ref[pl.ds(0, mem, stride=tiles), :], ref[pl.ds(tiles - 1, mem, stride=tiles), :])
+        for ref in fields
+    )
+    zonal, merid = (
+        jnp.broadcast_to(outermost(ref[:, :LANES], ref[:, end:]), (mem // 2, LANES))
+        for ref in courants
+    )
+    late = row_of((TILE, LANES)) >= STEPS
+    for i, parts in enumerate(((h, u), (v, zonal, merid))):
+        turned = jnp.concatenate(parts, axis=0).T
+        both = jnp.where(late, turned[LANES - TILE :], turned[:TILE])
+        edge_ref[i] = pltpu.roll(both, STEPS, 0)
+
+
+def blocks_kernel(groups, strips, width, mem, *refs):
+    h_ref, u_ref, v_ref, zonal_ref, merid_ref = refs[:5]
+    send_refs, (pair_ref, single_ref) = refs[5 : 5 + strips], refs[5 + strips :]
     tiles = h_ref.shape[0] // mem
     columns = tiles * LANES
-    zero = jnp.zeros((TILE, LANES), jnp.float32)
+    shape = (TILE, LANES)
+    zero = jnp.zeros(shape, jnp.float32)
     for ref in (pair_ref, single_ref):
         ref[0:TILE, :] = zero
         ref[columns : columns + TILE, :] = zero
-    for copy in copies[:5]:
-        copy.wait()
     for t in range(tiles):
         rows = pl.ds(t, mem, stride=tiles)
         lanes = slice(t * LANES, (t + 1) * LANES)
@@ -129,48 +152,52 @@
         place = slice(STEPS + t * LANES, STEPS + (t + 1) * LANES)
         pair_ref[place, :] = pair.T
         single_ref[place, :] = single.T
-    early = row_of((TILE, LANES)) < STEPS
-    for i, ref in enumerate((pair_ref, single_ref)):
-        edge_ref[i] = jnp.where(early, ref[columns : columns + TILE, :], ref[0:TILE, :])
-    for copy in copies[5:]:
-        copy.wait()
-    for q in range(REG_DEV):
-        live_ref[q] = jnp.full(live_ref.shape[1:], count_ref[q], jnp.int32)
-
-
-def blocks_kernel(groups, strips, width, pair_ref, single_ref, west_ref, east_ref, *refs):
-    send_refs = refs[-strips:]
     me = lax.axis_index("region")
-    shape = (TILE, LANES)
-    early = row_of(shape) < STEPS
     part = lane_of(shape) % (HALF // 2)
     span = 3 * TILE
     for s, send_ref in enumerate(send_refs):
         owner = me ^ s
-        first, last = early & (owner == 0), ~early & (owner == strips - 1)
-        courant = jnp.zeros(shape, jnp.float32)
+        courant = zero
         for p in range(groups // 2):
             for j in range(3):
                 pairs, singles = [], []
                 for group in (2 * p, 2 * p + 1):
                     start = pl.multiple_of(width * (group * strips + owner) + TILE * j, TILE)
-                    pair = pair_ref[pl.ds(start, TILE), :]
-                    single = single_ref[pl.ds(start, TILE), :]
-                    if group == 0 and j == 0:
-                        pair = jnp.where(first, west_ref[0], pair)
-                        single = jnp.where(first, west_ref[1], single)
-                    if group == groups - 1 and j == 2:
-                        pair = jnp.where(last, east_ref[0], pair)
-                        single = jnp.where(last, east_ref[1], single)
-                    pairs.append(pair)
-                    singles.append(single)
-                    courant = jnp.where(part == 3 * group + j, single, courant)
+                    pairs.append(pair_ref[pl.ds(start, TILE), :])
+                    singles.append(single_ref[pl.ds(start, TILE), :])
+                    courant = jnp.where(part == 3 * group + j, singles[-1], courant)
                 place = 3 * span * p + TILE * j
                 send_ref[place : place + TILE, :] = low_pair(*pairs)
                 send_ref[place + span : place + span + TILE, :] = high_pair(*pairs)
                 send_ref[place + 2 * span : place + 2 * span + TILE, :] = low_pair(*singles)
         place = 3 * span * (groups // 2)
         send_ref[place : place + TILE, :] = courant
+
+
+def wrap_kernel(groups, strips, west_ref, east_ref, *refs):
+    block_refs, send_refs = refs[:strips], refs[-strips:]
+    me = lax.axis_index("region")
+    shape = (TILE, LANES)
+    early = row_of(shape) < STEPS
+    low = lane_of(shape) < HALF
+    part = lane_of(shape) % (HALF // 2)
+    span = 3 * TILE
+    end = 3 * span * (groups // 2)
+    west = (west_ref[0], swapped(west_ref[0]), west_ref[1])
+    east = (swapped(east_ref[0]), east_ref[0], swapped(east_ref[1]))
+    for s in range(strips):
+        first, last = early & (me ^ s == 0), ~early & (me ^ s == strips - 1)
+        for i in range(3):
+            for place, mask, value in (
+                (span * i, first & low, west[i]),
+                (end - 3 * span + span * i + 2 * TILE, last & ~low, east[i]),
+            ):
+                tile = block_refs[s][place : place + TILE, :]
+                send_refs[s][place : place + TILE, :] = jnp.where(mask, value, tile)
+        tile = block_refs[s][end : end + TILE, :]
+        tile = jnp.where(first & ~low & (part == 0), west_ref[1], tile)
+        tile = jnp.where(last & ~low & (part == 3 * groups - 1), east_ref[1], tile)
+        send_refs[s][end : end + TILE, :] = tile
 
 
 def forecast_kernel(groups, strips, width, *refs):
@@ -246,7 +273,9 @@
             x_ref[q, :, lanes] = tile
 
 
-def observe_kernel(live_ref, index_ref, weight_ref, value_ref, var_ref, info_ref, pull_ref):
+def observe_kernel(count_ref, index_ref, weight_ref, value_ref, var_ref, ctrl_ref, *refs):
+    info_ref, pull_ref, near_ref = refs
+    near_ref[...] = ctrl_ref[...]
     states, padded = info_ref.shape[1:]
     obs = index_ref.shape[2]
     for q in range(REG_DEV):
@@ -255,7 +284,7 @@
         for j in range(index_ref.shape[1]):
             hit = state == index_ref[q, j : j + 1, :]
             operator = operator + jnp.where(hit, weight_ref[q, j : j + 1, :], 0.0)
-        live = lane_of((1, obs)) < live_ref[q, 0:1, 0:1]
+        live = lane_of((1, obs)) < count_ref[q]
         inverse = jnp.where(live, 1.0 / var_ref[q : q + 1, :], 0.0)
         scaled = operator * inverse
         info_ref[q] = lax.dot_general(
@@ -454,7 +483,7 @@
     return mean_state + increment + moved, increment
 
 
-def call(kernel, out_shape, specs, scratch=(), cost=None, place=VMEM):
+def call(kernel, out_shape, specs, scratch=(), cost=None, place=VMEM, aliases=None):
     many = isinstance(out_shape, tuple)
     return pl.pallas_call(
         kernel,
@@ -463,6 +492,7 @@
         out_specs=tuple(place for _ in out_shape) if many else place,
         scratch_shapes=scratch,
         cost_estimate=cost,
+        input_output_aliases=aliases or {},
         compiler_params=pltpu.CompilerParams(vmem_limit_bytes=GRANT),
     )
 
@@ -528,56 +558,60 @@
     flat = (mem * columns // LANES, LANES)
     states = 3 * width * strips // REG_DEV
     small = states <= members and groups > 2
-    later = [fine_ctrl]
-    if small:
-        later += [obs_index.transpose(0, 2, 1), obs_weight.transpose(0, 2, 1), obs_value, obs_var]
-    pair, single, edge, live, ctrl, *seen = call(
-        functools.partial(turn_kernel, mem, len(later)),
-        (
-            near(columns + TILE, LANES),
-            near(columns + TILE, LANES),
-            near(2, TILE, LANES),
-            pltpu.VMEM((REG_DEV, TILE, LANES), jnp.int32),
-            *(pltpu.VMEM(array.shape, array.dtype) for array in later),
-        ),
-        [HBM] * (6 + len(later)),
-        scratch=[
-            *[pltpu.VMEM(flat, jnp.float32)] * 3,
-            *[pltpu.VMEM((1, columns), jnp.float32)] * 2,
-            pltpu.SMEM((REG_DEV,), jnp.int32),
-            pltpu.SemaphoreType.DMA((6 + len(later),)),
-        ],
-    )(
-        far(sample_surface_elevation.reshape(flat)),
-        far(sample_zonal_current.reshape(flat)),
-        far(sample_meridional_current.reshape(flat)),
-        far(zonal_edge_layer_courant),
-        far(meridional_edge_layer_courant),
-        far(obs_count),
-        *(far(array) for array in later),
-    )
+    inputs = [
+        sample_surface_elevation.reshape(flat),
+        sample_zonal_current.reshape(flat),
+        sample_meridional_current.reshape(flat),
+        zonal_edge_layer_courant,
+        meridional_edge_layer_courant,
+    ]
+    edge, *taken = call(
+        functools.partial(edge_kernel, mem),
+        (near(2, TILE, LANES), *(near(*array.shape) for array in inputs)),
+        [HBM] * len(inputs),
+        scratch=[pltpu.SemaphoreType.DMA((len(inputs),))],
+    )(*(far(array) for array in inputs))
     from_west = passed_along(edge, "fine", 1)
     from_east = from_west if lax.axis_size("fine") == 2 else passed_along(edge, "fine", -1)
-    ahead = []
+    ctrl = fine_ctrl
     if small:
         padded = -(-states // LANES) * LANES
         obs = obs_value.shape[1]
-        info, pull = call(
+        info, pull, ctrl = call(
             observe_kernel,
-            (near(REG_DEV, states, padded), near(REG_DEV, states, LANES)),
-            [VMEM] * 5,
+            (
+                near(REG_DEV, states, padded),
+                near(REG_DEV, states, LANES),
+                near(*fine_ctrl.shape),
+            ),
+            [SMEM] + [VMEM] * 5,
             cost=pl.CostEstimate(
                 flops=12 * REG_DEV * padded * padded * obs, bytes_accessed=1 << 20, transcendentals=0
             ),
-        )(kept(live), *(kept(array) for array in seen))
-        ahead = [kept(pull)]
+        )(
+            far(obs_count),
+            far(obs_index.transpose(0, 2, 1)),
+            far(obs_weight.transpose(0, 2, 1)),
+            far(obs_value),
+            far(obs_var),
+            far(fine_ctrl),
+        )
     layout = (groups, strips, width)
     span = width + 2 * STEPS
+    blocks = tuple([near(3 * span * (groups // 2) + TILE, LANES)] * strips)
     out = call(
-        functools.partial(blocks_kernel, *layout),
-        tuple([near(3 * span * (groups // 2) + TILE, LANES)] * strips),
-        [VMEM] * (4 + len(ahead)),
-    )(kept(pair), kept(single), kept(from_west), kept(from_east), *ahead)
+        functools.partial(blocks_kernel, *layout, mem),
+        blocks,
+        [VMEM] * 5,
+        scratch=[pltpu.VMEM((columns + TILE, LANES), jnp.float32)] * 2,
+        cost=pl.CostEstimate(flops=1 << 20, bytes_accessed=1 << 20, transcendentals=0),
+    )(*(kept(array) for array in taken))
+    out = call(
+        functools.partial(wrap_kernel, groups, strips),
+        blocks,
+        [VMEM] * (2 + strips),
+        aliases={2 + s: s for s in range(strips)},
+    )(kept(from_west), kept(from_east), *(kept(block) for block in out))
     got = swapped_blocks(out, "region")
     turned = call(
         functools.partial(forecast_kernel, *layout),

time: 38 us -> 37.9 us (level)
  waiting for transfers between devices: 9.21 us -> 8.2 us
  Pallas kernels: 6.92 us -> 7.74 us
    ppermute x6, waiting for transfers between devices: 9.09 us -> 7.65 us  [swapped_blocks(): moved.append(lax.ppermute(blocks[s], axis, routes[s]))]
    pallas_call x1, Pallas kernels: 0.7 us -> 1.43 us  [shards(): call(observe_kernel, (near(REG_DEV, states, padded), near(REG_DEV, states...]
    ppermute x1, waiting for transfers between devices: 0.12 us -> 0.55 us  [passed_along(): return lax.ppermute(block, axis, route)]
    pallas_call x2 -> x3, Pallas kernels: 1.32 us -> 1.41 us  [the longest x1 1.06 us: shards(): call(functools.partial(edge_kernel, mem), (near(2, TILE, LANES), *(near(*...]
  transfers between devices with their start and end apart: 7 -> 7, of which waited for: 7 -> 7; matrix products, arithmetic and copies ran while one was open for 0% -> 0% of each run, Pallas kernels for 3% -> 6%
where the time goes in v4:
time: 37.9 us; the launch traced here: 37.6 us
  blocking collectives  11.6 us (31%)
  starting transfers between devices  9.39 us (25%)
  waiting for transfers between devices  8.2 us (22%)
  Pallas kernels  7.74 us (20%)
  between operations  0.69 us (2%)
    all_to_all x1, blocking collectives, exchanged(): lax.all_to_all(dense, axes, split_axis=0, concat_axis=0, tiled=True)  11.6 us
    ppermute x6, starting transfers between devices, swapped_blocks(): moved.append(lax.ppermute(blocks[s], axis, routes[s]))  8.83 us
    ppermute x6, waiting for transfers between devices, swapped_blocks(): moved.append(lax.ppermute(blocks[s], axis, routes[s]))  7.65 us
    pallas_call x1, Pallas kernels, shards(): call(functools.partial(region_kernel, *layout), back_shape, [VMEM] * (gro...  3.13 us
    pallas_call x1, Pallas kernels, shards(): call(observe_kernel, (near(REG_DEV, states, padded), near(REG_DEV, states...  1.43 us
    pallas_call x1, Pallas kernels, shards(): call(functools.partial(edge_kernel, mem), (near(2, TILE, LANES), *(near(*...  1.06 us
    pallas_call x1, Pallas kernels, shards(): call(functools.partial(home_kernel, mem, strips, width), (f32(*flat), f32...  0.94 us
  transfers between devices with their start and end apart: 7, of which 7 were waited for; matrix products, arithmetic and copies ran while one was open for 0% of the time, Pallas kernels for 6%

profile of v4, /device:TPU:0, one launch (start us, length us, event | category | flops | bytes accessed | tf_op | source)
XLA Modules:
  0.0 37.6 jit_solution(13758679585012769853)
XLA Ops:
  0.6 1.1 %shard_map.138 = (f32[2,8,128]{2,1,0:T(8,128)S(1)}, f32[128,128]{1,0:T(8,128)S(1)}, f32[128,128]{1,0:T(8,128)S(1)}, f32[128,128]{1,0:T(8,128)S(1)}, f32[1,256]{1,0:T(1,128)S(1)}, /*index=5*/f32[1,256]{1,0:T(1,128)S(1)}) custom-call(f32[128,128]{1,0:T(8,128)} %bitcast.12, f32[128,128]{1,0:T(8,128)} %bitcast.13, f32[128,128]{1,0:T(8,128)} %bitcast.14, ...), custom_call_target="tpu_custom_call" | custom-call | tf_op jit(solution)/shard_map/pallas_call | solution.py:568
  1.7 0.6 %collective-permute-start = (f32[2,8,128]{2,1,0:T(8,128)S(1)}, f32[2,8,128]{2,1,0:T(8,128)S(1)}, u32[]{:S(2)}, u32[]{:S(2)}) collective-permute-start(f32[2,8,128]{2,1,0:T(8,128)S(1)} %get-tuple-element.31), channel_id=1, source_target_pairs={{1,0},{0,1},{3,2},{2,3},{5,4},{4,5},{7,6},{6,7},{9,8},{8,9},{11,10... | collective-permute-start | bytes 24584 | tf_op jit(solution)/shard_map/ppermute | solution.py:31
  2.3 0.3 shard_map.139
  2.5 0.5 %collective-permute-done.west_ref.east_ref = f32[2,8,128]{2,1,0:T(8,128)S(1)} collective-permute-done((f32[2,8,128]{2,1,0:T(8,128)S(1)}, f32[2,8,128]{2,1,0:T(8,128)S(1)}, u32[]{:S(2)}, u32[]{:S(2)}) %collective-permute-start) | collective-permute-done | bytes 8224 | tf_op jit(solution)/shard_map/ppermute | solution.py:31
  3.1 0.1 shard_map.140
  3.2 2.8 %collective-permute-start.1 = (f32[152,128]{1,0:T(8,128)S(1)}, f32[152,128]{1,0:T(8,128)S(1)}, u32[]{:S(2)}, u32[]{:S(2)}) collective-permute-start(f32[152,128]{1,0:T(8,128)S(1)} %get-tuple-element.42), channel_id=1, source_target_pairs={{0,2},{2,0},{4,6},{6,4},{1,3},{3,1},{5,7},{7,5},{8,10},{10,8},{12,... | collective-permute-start | bytes 233480 | tf_op jit(solution)/shard_map/ppermute | solution.py:506
  6.0 1.5 %collective-permute-start.2 = (f32[152,128]{1,0:T(8,128)S(1)}, f32[152,128]{1,0:T(8,128)S(1)}, u32[]{:S(2)}, u32[]{:S(2)}) collective-permute-start(f32[152,128]{1,0:T(8,128)S(1)} %get-tuple-element.43), channel_id=1, source_target_pairs={{0,4},{2,6},{4,0},{6,2},{1,5},{3,7},{5,1},{7,3},{8,12},{10,14},{12... | collective-permute-start | bytes 233480 | tf_op jit(solution)/shard_map/ppermute | solution.py:506
  7.5 0.0 collective-permute-start.3
  7.5 1.1 %collective-permute-done.1.refs_1_ = f32[152,128]{1,0:T(8,128)S(1)} collective-permute-done((f32[152,128]{1,0:T(8,128)S(1)}, f32[152,128]{1,0:T(8,128)S(1)}, u32[]{:S(2)}, u32[]{:S(2)}) %collective-permute-start.1) | collective-permute-done | bytes 77856 | tf_op jit(solution)/shard_map/ppermute | solution.py:506
  8.7 2.4 %collective-permute-done.2.refs_2_ = f32[152,128]{1,0:T(8,128)S(1)} collective-permute-done((f32[152,128]{1,0:T(8,128)S(1)}, f32[152,128]{1,0:T(8,128)S(1)}, u32[]{:S(2)}, u32[]{:S(2)}) %collective-permute-start.2) | collective-permute-done | bytes 77856 | tf_op jit(solution)/shard_map/ppermute | solution.py:506
  11.1 1.7 %collective-permute-done.3.refs_3_ = f32[152,128]{1,0:T(8,128)S(1)} collective-permute-done((f32[152,128]{1,0:T(8,128)S(1)}, f32[152,128]{1,0:T(8,128)S(1)}, u32[]{:S(2)}, u32[]{:S(2)}) %collective-permute-start.3) | collective-permute-done | bytes 77856 | tf_op jit(solution)/shard_map/ppermute | solution.py:506
  12.8 0.4 %shard_map.141 = (f32[96,128]{1,0:T(8,128)S(1)}, f32[96,128]{1,0:T(8,128)S(1)}, f32[96,128]{1,0:T(8,128)S(1)}, f32[96,128]{1,0:T(8,128)S(1)}) custom-call(f32[152,128]{1,0:T(8,128)S(1)} %get-tuple-element.41.refs_0_, f32[152,128]{1,0:T(8,128)S(1)} %collective-permute-done.1.refs_1_, f32[152,128]{1,0:T(8,128)S(1)} %collective-permute-done.2.refs_2_, ...), custom_call_target="tpu_custom_call" | custom-call | tf_op jit(solution)/shard_map/pallas_call | solution.py:616
  13.3 3.7 %collective-permute-start.6 = (f32[96,128]{1,0:T(8,128)S(1)}, f32[96,128]{1,0:T(8,128)S(1)}, u32[]{:S(2)}, u32[]{:S(2)}) collective-permute-start(f32[96,128]{1,0:T(8,128)S(1)} %get-tuple-element.48), channel_id=1, source_target_pairs={{0,24},{8,16},{16,8},{24,0},{1,25},{9,17},{17,9},{25,1},{2,26},{10... | collective-permute-start | bytes 147464 | tf_op jit(solution)/shard_map/ppermute | solution.py:506
  16.9 0.0 collective-permute-start.4
  16.9 0.8 %collective-permute-start.5 = (f32[96,128]{1,0:T(8,128)S(1)}, f32[96,128]{1,0:T(8,128)S(1)}, u32[]{:S(2)}, u32[]{:S(2)}) collective-permute-start(f32[96,128]{1,0:T(8,128)S(1)} %get-tuple-element.47), channel_id=1, source_target_pairs={{0,16},{8,24},{16,0},{24,8},{1,17},{9,25},{17,1},{25,9},{2,18},{10... | collective-permute-start | bytes 147464 | tf_op jit(solution)/shard_map/ppermute | solution.py:506
  17.7 1.4 %shard_map.143 = (f32[2,96,128]{2,1,0:T(8,128)S(1)}, f32[2,96,128]{2,1,0:T(8,128)S(1)}, f32[3,2,1,128]{3,2,1,0:T(1,128)S(1)}) custom-call(s32[2]{0:T(128)} %count_ref.1, s32[2,4,512]{2,1,0:T(4,128)} %bitcast.18, f32[2,4,512]{2,1,0:T(4,128)} %bitcast.19, f32[2,512]{1,0:T(2,128)} %value_ref.1, f32[2,512]{1,0:T(2,128)} %var_ref.1, f32[3,2,1,128]{3,2,1,0:T(1,128)} %ctrl_ref.1), custom_call_target="tpu_custom_call" | custom-call | flops 201326592 | bytes 1048576 | tf_op jit(solution)/shard_map/pallas_call | solution.py:580
  19.2 0.2 collective-permute-done.6.odd_ref.refs_3_
  19.3 0.4 %shard_map.142 = (f32[2,96,128]{2,1,0:T(8,128)S(1)}, f32[2,96,128]{2,1,0:T(8,128)S(1)}) custom-call(f32[96,128]{1,0:T(8,128)S(1)} %get-tuple-element.45.even_ref.refs_0_, f32[96,128]{1,0:T(8,128)S(1)} %collective-permute-done.6.odd_ref.refs_3_), custom_call_target="tpu_custom_call" | custom-call | flops 33554432 | bytes 262144 | tf_op jit(solution)/shard_map/pallas_call | solution.py:629
  19.7 1.3 %collective-permute-done.4.refs_1_ = f32[96,128]{1,0:T(8,128)S(1)} collective-permute-done((f32[96,128]{1,0:T(8,128)S(1)}, f32[96,128]{1,0:T(8,128)S(1)}, u32[]{:S(2)}, u32[]{:S(2)}) %collective-permute-start.4) | collective-permute-done | bytes 49184 | tf_op jit(solution)/shard_map/ppermute | solution.py:506
  21.0 0.9 %collective-permute-done.5.refs_2_ = f32[96,128]{1,0:T(8,128)S(1)} collective-permute-done((f32[96,128]{1,0:T(8,128)S(1)}, f32[96,128]{1,0:T(8,128)S(1)}, u32[]{:S(2)}, u32[]{:S(2)}) %collective-permute-start.5) | collective-permute-done | bytes 49184 | tf_op jit(solution)/shard_map/ppermute | solution.py:506
  21.9 3.1 %shard_map.144 = f32[400,128]{1,0:T(8,128)S(1)} custom-call(f32[96,128]{1,0:T(8,128)S(1)} %get-tuple-element.45.even_ref.refs_0_, f32[96,128]{1,0:T(8,128)S(1)} %collective-permute-done.4.refs_1_, f32[96,128]{1,0:T(8,128)S(1)} %collective-permute-done.5.refs_2_, f32[96,128]{1,0:T(8,128)S(1)} %collective-permute-done.6.odd_ref.refs_3_, ...), custom_call_target="tpu_custom_call" | custom-call | tf_op jit(solution)/shard_map/pallas_call | solution.py:637
  25.1 11.6 %all_to_all.5 = f32[16,25,1,128]{3,2,1,0:T(1,128)S(1)} all-to-all(f32[16,25,1,128]{3,2,1,0:T(1,128)S(1)} %bitcast.10), channel_id=1, replica_groups=mesh['member'=4,'region'=4,'fine'=2] {'member','region'}, dimensions={0} | all-to-all | bytes 409600 | tf_op jit(solution)/shard_map/all_to_all | solution.py:515
  36.6 0.9 %shard_map.145 = (f32[128,128]{1,0:T(8,128)}, f32[128,128]{1,0:T(8,128)}, f32[128,128]{1,0:T(8,128)}, f32[3,2,1,128]{3,2,1,0:T(1,128)}) custom-call(f32[400,128]{1,0:T(8,128)S(1)} %bitcast.11, f32[3,2,1,128]{3,2,1,0:T(1,128)S(1)} %get-tuple-element.53.ctrl_ref), custom_call_target="tpu_custom_call" | custom-call | tf_op jit(solution)/shard_map/pallas_call | solution.py:661
Async XLA Ops:
  1.7 1.4 %collective-permute-start = (f32[2,8,128]{2,1,0:T(8,128)S(1)}, f32[2,8,128]{2,1,0:T(8,128)S(1)}, u32[]{:S(2)}, u32[]{:S(2)}) collective-permute-start(f32[2,8,128]{2,1,0:T(8,128)S(1)} %get-tuple-element.31), channel_id=1, source_target_pairs={{1,0},{0,1},{3,2},{2,3},{5,4},{4,5},{7,6},{6,7},{9,8},{8,9},{11,10... | collective-permute-start | bytes 24584 | tf_op jit(solution)/shard_map/ppermute | solution.py:31
  3.2 5.5 %collective-permute-start.1 = (f32[152,128]{1,0:T(8,128)S(1)}, f32[152,128]{1,0:T(8,128)S(1)}, u32[]{:S(2)}, u32[]{:S(2)}) collective-permute-start(f32[152,128]{1,0:T(8,128)S(1)} %get-tuple-element.42), channel_id=1, source_target_pairs={{0,2},{2,0},{4,6},{6,4},{1,3},{3,1},{5,7},{7,5},{8,10},{10,8},{12,... | collective-permute-start | bytes 233480 | tf_op jit(solution)/shard_map/ppermute | solution.py:506
  6.0 5.1 %collective-permute-start.2 = (f32[152,128]{1,0:T(8,128)S(1)}, f32[152,128]{1,0:T(8,128)S(1)}, u32[]{:S(2)}, u32[]{:S(2)}) collective-permute-start(f32[152,128]{1,0:T(8,128)S(1)} %get-tuple-element.43), channel_id=1, source_target_pairs={{0,4},{2,6},{4,0},{6,2},{1,5},{3,7},{5,1},{7,3},{8,12},{10,14},{12... | collective-permute-start | bytes 233480 | tf_op jit(solution)/shard_map/ppermute | solution.py:506
  7.5 5.3 %collective-permute-start.3 = (f32[152,128]{1,0:T(8,128)S(1)}, f32[152,128]{1,0:T(8,128)S(1)}, u32[]{:S(2)}, u32[]{:S(2)}) collective-permute-start(f32[152,128]{1,0:T(8,128)S(1)} %get-tuple-element.44), channel_id=1, source_target_pairs={{0,6},{2,4},{4,2},{6,0},{1,7},{3,5},{5,3},{7,1},{8,14},{10,12},{12... | collective-permute-start | bytes 233480 | tf_op jit(solution)/shard_map/ppermute | solution.py:506
  13.3 6.1 %collective-permute-start.6 = (f32[96,128]{1,0:T(8,128)S(1)}, f32[96,128]{1,0:T(8,128)S(1)}, u32[]{:S(2)}, u32[]{:S(2)}) collective-permute-start(f32[96,128]{1,0:T(8,128)S(1)} %get-tuple-element.48), channel_id=1, source_target_pairs={{0,24},{8,16},{16,8},{24,0},{1,25},{9,17},{17,9},{25,1},{2,26},{10... | collective-permute-start | bytes 147464 | tf_op jit(solution)/shard_map/ppermute | solution.py:506
  16.9 4.1 %collective-permute-start.4 = (f32[96,128]{1,0:T(8,128)S(1)}, f32[96,128]{1,0:T(8,128)S(1)}, u32[]{:S(2)}, u32[]{:S(2)}) collective-permute-start(f32[96,128]{1,0:T(8,128)S(1)} %get-tuple-element.46), channel_id=1, source_target_pairs={{0,8},{8,0},{16,24},{24,16},{1,9},{9,1},{17,25},{25,17},{2,10},{10... | collective-permute-start | bytes 147464 | tf_op jit(solution)/shard_map/ppermute | solution.py:506
  16.9 5.0 %collective-permute-start.5 = (f32[96,128]{1,0:T(8,128)S(1)}, f32[96,128]{1,0:T(8,128)S(1)}, u32[]{:S(2)}, u32[]{:S(2)}) collective-permute-start(f32[96,128]{1,0:T(8,128)S(1)} %get-tuple-element.47), channel_id=1, source_target_pairs={{0,16},{8,24},{16,0},{24,8},{1,17},{9,25},{17,1},{25,9},{2,18},{10... | collective-permute-start | bytes 147464 | tf_op jit(solution)/shard_map/ppermute | solution.py:506
